TPU v7x, 32 devices: a whole 2x2x4 slice. The times are simulated.
32 devices in a mesh: groups: 1, expert: 8 (over z, core), dp: 4 (over y, x).
Axes of the slice: x: 2, y: 2, z: 4, core: 2. Of those that a mesh axis runs over, the one named last changes fastest.
Arguments:
- tokens: bfloat16 [128, 4096], P(('groups', 'expert', 'dp')), may hold values from -6 to 6
- expert_ids: int32 [128, 2], P(('groups', 'expert', 'dp')), may hold values from 0 to 7, as said below
- gate_weights: bfloat16 [128, 2], P(('groups', 'expert', 'dp')), may hold values from 0.099609375 to 1
- placement: int32 [2, 2], P('groups'), may hold values from 0 to 7, as said below
- w_gate: bfloat16 [8, 1536, 4096], P('expert', 'dp'), may hold values from -0.09375 to 0.09375
- w_up: bfloat16 [8, 1536, 4096], P('expert', 'dp'), may hold values from -0.09375 to 0.09375
- w_down: bfloat16 [8, 1536, 4096], P('expert', 'dp'), may hold values from -0.15625 to 0.15625
Outputs:
- mixed: bfloat16 [128, 4096], P(('groups', 'expert', 'dp'))
Inputs may be any that keep to these rules, and one draw needn't show every extreme that they name: `expert_ids`: each row names 2 different experts. In each aligned block of 16 rows (the tokens of one index of expert) no expert is named by more than 6 rows, and some expert is named by exactly that many. `placement`: row 0 holds 2 different experts; row 1 holds 2 different expert indices, none of which appears in row 0.
All inputs are finite; a program needn't handle non-finite values.
Results may differ from a plain program's by a relative error of at most 0.015.
Values may be sent and summed in bfloat16 or wider, within the bound.
A program may use at most 64 MiB of HBM per device.

v0:
```python
import functools

import jax
import jax.numpy as jnp
from jax import lax
from jax.experimental import pallas as pl
from jax.experimental.pallas import tpu as pltpu
from jax.sharding import PartitionSpec as P

MESH = pl.DeviceIdType.MESH
F32 = jnp.float32
BF16 = jnp.bfloat16


def each(count, step):
    if count <= 8:
        for i in range(count):
            step(i)
    else:
        def turn(i, carry):
            step(i)
            return carry

        lax.fori_loop(0, count, turn, 0)


def each_from(first, count, step):
    each(count - first, lambda i: step(i + first))


def kernel(experts, dp, topk, first, slots, padded,
           tok_hbm, ids_hbm, gates_hbm, placement_hbm, wg_hbm, wu_hbm, wd_hbm, out,
           tok, ids, gates, placement,
           wg, wu, wd, tok_s, tok_r, info_s, info_r, group_x, disp_s, rows_r, rows_f, part_f,
           part_s, part_r, back_s, back_r, wsel, mix_s,
           w_sem, s1, r1, si, ri, s2, r2, s3, r3, s4, r4, s5, r5, s6, r6):
    me_e = lax.axis_index("expert")
    me_j = lax.axis_index("dp")
    own, width = tok.shape
    block = width // dp
    group = own * dp
    pairs = group * topk
    lanes = info_s.shape[1]
    total = experts * padded

    if dp == 4:
        low, high = lax.rem(me_j, 2), me_j // 2
        across = (me_j, high * 2 + (1 - low), (1 - high) * 2 + low, (1 - high) * 2 + (1 - low))
        onward = backward = lambda s: across[s]
    else:
        onward = lambda s: lax.rem(me_j + s, dp)
        backward = lambda s: lax.rem(me_j + dp - s, dp)

    def to_dp(src, dst, send, recv, s):
        return pltpu.make_async_remote_copy(
            src_ref=src, dst_ref=dst, send_sem=send, recv_sem=recv,
            device_id={"dp": onward(s)}, device_id_type=MESH)

    def to_expert(src, dst, send, recv, shift):
        return pltpu.make_async_remote_copy(
            src_ref=src, dst_ref=dst, send_sem=send, recv_sem=recv,
            device_id={"expert": lax.rem(me_e + shift, experts)}, device_id_type=MESH)

    def cols(j):
        return pl.ds(pl.multiple_of(j * block, 128), block)

    barrier = pltpu.get_barrier_semaphore()
    for s in range(1, dp):
        pl.semaphore_signal(barrier, inc=1, device_id={"dp": onward(s)}, device_id_type=MESH)

    def greet(d):
        pl.semaphore_signal(barrier, inc=1, device_id={"expert": lax.rem(me_e + d, experts)}, device_id_type=MESH)

    each_from(1, experts, greet)

    pairs_of = ((ids_hbm, ids), (gates_hbm, gates), (placement_hbm, placement), (tok_hbm, tok),
                (wg_hbm, wg), (wu_hbm, wu), (wd_hbm, wd))
    loads = [pltpu.make_async_copy(a, b, w_sem.at[i]) for i, (a, b) in enumerate(pairs_of)]
    for load in loads:
        load.start()
    for load in loads[:4]:
        load.wait()
    loads = loads[4:]

    lane = lax.broadcasted_iota(jnp.int32, (8, lanes), 1)
    line = lax.broadcasted_iota(jnp.int32, (8, lanes), 0)
    id_f = ids[...].astype(F32)
    gate_f = gates[...].astype(F32)
    info = jnp.zeros((8, lanes), F32)
    for t in range(own):
        for k in range(topk):
            here = lane == (me_j * own + t) * topk + k
            value = jnp.where(line == 0, jnp.broadcast_to(id_f[k:k + 1, t:t + 1], (8, lanes)),
                              jnp.broadcast_to(gate_f[k:k + 1, t:t + 1], (8, lanes)))
            info = jnp.where(here, value, info)
    info_s[...] = info
    for s in range(1, dp):
        tok_s[s] = tok[:, cols(onward(s))]
    tok_r[me_j] = tok[:, cols(me_j)]

    pl.semaphore_wait(barrier, dp - 1 + experts - 1)

    for s in range(1, dp):
        to_dp(info_s, info_r.at[s], si.at[s], ri.at[s], s).start()
    for s in range(1, dp):
        to_dp(tok_s.at[s], tok_r.at[me_j], s1.at[s], r1.at[s], s).start()
    for s in range(1, dp):
        to_dp(info_s, info_r.at[s], si.at[s], ri.at[s], s).wait_recv()
        info = info + info_r[s]

    id_row = info[0:1, :]
    gate_row = info[1:2, :]
    at_row = lax.broadcasted_iota(jnp.int32, (pairs, lanes), 0)
    at_lane = lax.broadcasted_iota(jnp.int32, (pairs, lanes), 1)
    id_col = jnp.sum(jnp.where(at_row == at_lane, jnp.broadcast_to(id_row, (pairs, lanes)), 0.0),
                     axis=1, keepdims=True)
    same = jnp.broadcast_to(id_col, (pairs, lanes)) == jnp.broadcast_to(id_row, (pairs, lanes))
    rank = jnp.sum(jnp.where(same, jnp.where(at_row < at_lane, 1.0, 0.0), 0.0), axis=0, keepdims=True)
    limit = jnp.full((1, lanes), float(first), F32)
    listed = placement[...].astype(F32)
    for h in range(placement.shape[1]):
        limit = jnp.where(id_row == jnp.broadcast_to(listed[0:1, h:h + 1], (1, lanes)), float(slots), limit)
    dest = jnp.where(rank < limit, id_row * float(padded) + rank, -1.0)
    dest = jnp.where(lax.broadcasted_iota(jnp.int32, (1, lanes), 1) < pairs, dest, -1.0)
    pick = lax.broadcasted_iota(jnp.int32, (total, lanes), 0).astype(F32) == jnp.broadcast_to(dest, (total, lanes))
    pair_i = lax.broadcasted_iota(jnp.int32, (lanes, group), 0)
    token_i = lax.broadcasted_iota(jnp.int32, (lanes, group), 1) * topk
    fold = jnp.where(pair_i >= token_i, jnp.where(pair_i < token_i + topk, 1.0, 0.0), 0.0).astype(BF16)
    select = jnp.dot(jnp.where(pick, 1.0, 0.0).astype(BF16), fold, preferred_element_type=F32).astype(BF16)

    for s in range(1, dp):
        to_dp(tok_s.at[s], tok_r.at[backward(s)], s1.at[s], r1.at[s], s).wait_recv()
    for j in range(dp):
        group_x[j * own:(j + 1) * own, :] = tok_r[j].astype(F32)
    rows_f[...] = jnp.dot(select, group_x[...].astype(BF16), preferred_element_type=F32)

    def dispatch(d):
        e = lax.rem(me_e + d, experts)
        start = pl.multiple_of(e * padded, 8)
        disp_s[e] = rows_f[pl.ds(start, slots), :].astype(BF16)
        to_expert(disp_s.at[e], rows_r.at[me_j, me_e], s2.at[d], r2.at[d], d).start()

    each_from(1, experts, dispatch)
    rows_r[me_j, me_e] = rows_f[pl.ds(pl.multiple_of(me_e * padded, 8), slots), :].astype(BF16)

    relayed = dp == 4 and experts <= 8
    direct = (1, 2) if relayed else range(1, dp)

    def forward(d):
        g = lax.rem(me_e + experts - d, experts)
        for s in direct:
            to_dp(rows_r.at[me_j, g], rows_r.at[me_j, g], s3.at[s, d], r3.at[s, d], s).start()

    forward(0)
    wsel[...] = jnp.dot(jnp.where(pick, jnp.broadcast_to(gate_row, (total, lanes)), 0.0).astype(BF16), fold,
                        preferred_element_type=F32)


    def arrive(d):
        g = lax.rem(me_e + experts - d, experts)
        to_expert(disp_s.at[g], rows_r.at[me_j, g], s2.at[d], r2.at[d], d).wait_recv()
        forward(d)

    each_from(1, experts, arrive)

    loads[0].wait()
    loads[1].wait()
    contract = (((1,), (1,)), ((), ()))

    def first_of(d):
        return 1 + d % 2

    def relay(d):
        g = lax.rem(me_e + experts - d, experts)
        side = first_of(d)
        j = onward(side)
        to_dp(rows_r.at[j, g], rows_r.at[j, g], s3.at[side, d], r3.at[side, d], side).wait_recv()
        to_dp(rows_r.at[j, g], rows_r.at[j, g], s3.at[3, d], r3.at[3, d], 3 - side).start()

    gate = up = None
    for s in range(dp):
        j = backward(s)

        def take(d):
            g = lax.rem(me_e + experts - d, experts)
            if s > 0 and not (relayed and s == first_of(d)):
                to_dp(rows_r.at[j, g], rows_r.at[j, g], s3.at[s, d], r3.at[s, d], s).wait_recv()
            rows_f[pl.ds(pl.multiple_of(g * padded, 8), slots), :] = rows_r[j, g].astype(F32)

        each(experts, take)
        x = rows_f[...].astype(BF16)
        gate_part = lax.dot_general(x, wg[:, cols(j)], contract, preferred_element_type=F32)
        up_part = lax.dot_general(x, wu[:, cols(j)], contract, preferred_element_type=F32)
        gate = gate_part if gate is None else gate + gate_part
        up = up_part if up is None else up + up_part
        if relayed and s == 0:
            each(experts, relay)
    hidden = (gate / (1.0 + jnp.exp(-gate)) * up).astype(BF16)

    loads[2].wait()
    for s in reversed(range(dp)):
        j = onward(s)
        part_f[...] = jnp.dot(hidden, wd[:, cols(j)], preferred_element_type=F32)
        target = part_s if s > 0 else part_r

        def split(d):
            g = lax.rem(me_e + d, experts)
            start = pl.multiple_of(g * padded, 8)
            target[s, g] = part_f[pl.ds(start, slots), :].astype(BF16)
            if s > 0:
                to_dp(part_s.at[s, g], part_r.at[s, g], s4.at[s, d], r4.at[s, d], s).start()

        each_from(1, experts, split)
        split(0)

    def summed(d):
        g = lax.rem(me_e + d, experts)
        for s in range(1, dp):
            to_dp(part_s.at[s, g], part_r.at[s, g], s4.at[s, d], r4.at[s, d], s).wait_recv()
        value = part_r[0, g].astype(F32)
        for s in range(1, dp):
            value = value + part_r[s, g].astype(F32)
        return value.astype(BF16)

    def give(d):
        g = lax.rem(me_e + d, experts)
        back_s[g] = summed(d)
        to_expert(back_s.at[g], back_r.at[me_e], s5.at[d], r5.at[d], d).start()

    each_from(1, experts, give)
    back_r[me_e] = summed(0)

    def collect(d):
        e = lax.rem(me_e + experts - d, experts)
        to_expert(back_s.at[e], back_r.at[e], s5.at[d], r5.at[d], d).wait_recv()

    each_from(1, experts, collect)

    def place(e):
        rows_f[pl.ds(e * padded, slots), :] = back_r[e].astype(F32)

    each(experts, place)
    group_x[...] = lax.dot_general(wsel[...].astype(BF16), rows_f[...].astype(BF16), (((0,), (0,)), ((), ())),
                                   preferred_element_type=F32)
    for j in range(dp):
        mix_s[j] = group_x[j * own:(j + 1) * own, :].astype(BF16)
    for s in reversed(range(1, dp)):
        to_dp(mix_s.at[onward(s)], out.at[:, cols(me_j)], s6.at[s], r6.at[s], s).start()
    kept = pltpu.make_async_copy(mix_s.at[me_j], out.at[:, cols(me_j)], s6.at[0])
    kept.start()
    kept.wait()
    for s in range(1, dp):
        j = backward(s)
        to_dp(mix_s.at[j], out.at[:, cols(j)], s6.at[s], r6.at[s], s).wait_recv()

    for s in range(1, dp):
        to_dp(info_s, info_r.at[s], si.at[s], ri.at[s], s).wait_send()
        to_dp(tok_s.at[s], tok_r.at[me_j], s1.at[s], r1.at[s], s).wait_send()
        to_dp(mix_s.at[onward(s)], out.at[:, cols(me_j)], s6.at[s], r6.at[s], s).wait_send()

    def left(d):
        g = lax.rem(me_e + experts - d, experts)
        for s in range(1, dp):
            to_dp(rows_r.at[me_j, g], rows_r.at[me_j, g], s3.at[s, d], r3.at[s, d], s).wait_send()
            to_dp(part_s.at[s, g], part_r.at[s, g], s4.at[s, d], r4.at[s, d], s).wait_send()

    def left_expert(d):
        e = lax.rem(me_e + d, experts)
        to_expert(disp_s.at[e], rows_r.at[me_j, me_e], s2.at[d], r2.at[d], d).wait_send()
        to_expert(back_s.at[e], back_r.at[me_e], s5.at[d], r5.at[d], d).wait_send()

    each(experts, left)
    each_from(1, experts, left_expert)


def body(tokens, expert_ids, gate_weights, placement, w_gate, w_up, w_down):
    experts = lax.axis_size("expert")
    dp = lax.axis_size("dp")
    own, width = tokens.shape
    topk = expert_ids.shape[1]
    group = own * dp
    first = max(2, group * topk // experts)
    slots = first + max(1, first // 2)
    padded = -(-slots // 8) * 8
    lanes = -(-group * topk // 128) * 128
    block = width // dp
    units = w_gate.shape[1]
    total = experts * padded
    hbm = pl.BlockSpec(memory_space=pl.ANY)
    dma = pltpu.SemaphoreType.DMA
    return pl.pallas_call(
        functools.partial(kernel, experts, dp, topk, first, slots, padded),
        out_shape=jax.ShapeDtypeStruct((own, width), BF16),
        in_specs=[hbm] * 7,
        out_specs=hbm,
        scratch_shapes=[
            pltpu.VMEM((own, width), BF16),
            pltpu.VMEM((topk, own), jnp.int32),
            pltpu.VMEM((topk, own), BF16),
            pltpu.VMEM(placement.shape, jnp.int32),
            pltpu.VMEM((units, width), BF16),
            pltpu.VMEM((units, width), BF16),
            pltpu.VMEM((units, width), BF16),
            pltpu.VMEM((dp, own, block), BF16),
            pltpu.VMEM((dp, own, block), BF16),
            pltpu.VMEM((8, lanes), F32),
            pltpu.VMEM((dp, 8, lanes), F32),
            pltpu.VMEM((group, block), F32),
            pltpu.VMEM((experts, slots, block), BF16),
            pltpu.VMEM((dp, experts, slots, block), BF16),
            pltpu.VMEM((total, block), F32),
            pltpu.VMEM((total, block), F32),
            pltpu.VMEM((dp, experts, slots, block), BF16),
            pltpu.VMEM((dp, experts, slots, block), BF16),
            pltpu.VMEM((experts, slots, block), BF16),
            pltpu.VMEM((experts, slots, block), BF16),
            pltpu.VMEM((total, group), F32),
            pltpu.VMEM((dp, own, block), BF16),
            dma((7,)),
            dma((dp,)), dma((dp,)), dma((dp,)), dma((dp,)),
            dma((experts,)), dma((experts,)),
            dma((dp, experts)), dma((dp, experts)),
            dma((dp, experts)), dma((dp, experts)),
            dma((experts,)), dma((experts,)),
            dma((dp,)), dma((dp,)),
        ],
        compiler_params=pltpu.CompilerParams(
            collective_id=0, has_side_effects=True, vmem_limit_bytes=56 << 20
        ),
    )(tokens, expert_ids.T, gate_weights.T, placement, w_gate[0], w_up[0], w_down[0])


def solution(mesh):
    placed = (
        P(("groups", "expert", "dp"), None),
        P(("groups", "expert", "dp"), None),
        P(("groups", "expert", "dp"), None),
        P("groups", None),
        P("expert", "dp", None),
        P("expert", "dp", None),
        P("expert", "dp", None),
    )
    return jax.shard_map(
        body,
        mesh=mesh,
        in_specs=placed,
        out_specs=P(("groups", "expert", "dp"), None),
        check_vma=False,
    )
```

profile of v0, /device:TPU:0, one launch (start us, length us, event | category | flops | bytes accessed | tf_op | source)
XLA Modules:
  0.0 36.3 jit_solution(16238196882760517996)
XLA Ops:
  0.0 34.9 %shard_map.73 = bf16[4,4096]{1,0:T(4,128)(2,1)} custom-call(bf16[4,4096]{1,0:T(4,128)(2,1)} %tok_hbm.1, s32[2,4]{1,0:T(2,128)} %bitcast.8, bf16[2,4]{1,0:T(2,128)(2,1)} %bitcast.9, s32[2,2]{1,0:T(2,128)} %placement_hbm.1, bf16[384,4096]{1,0:T(8,128)(2,1)} %bitcast.5, bf16[384,4096]{1,0:T(8,128)(2,1)} %bitcast.6, bf16[384,4096]{1,0:T(8,128)(2,1)} %bitcast.7), custom_call_target="tpu_custom_call" | custom-call | tf_op jit(solution)/shard_map/pallas_call | solution.py:291
  34.9 1.4 %copy.9 = bf16[4,4096]{1,0:T(4,128)(2,1)} copy(bf16[4,4096]{1,0:T(4,128)(2,1)} %shard_map.73) | data formatting | bytes 65536
where the time goes:
time: 36.4 us; the launch traced here: 36.3 us
  Pallas kernels  34.9 us (96%)
  local copies, waits for them, and re-layouts  1.39 us (4%)
    pallas_call x1, Pallas kernels, body(): pl.pallas_call(functools.partial(kernel, experts, dp, topk, first, slots,...  34.9 us
    unnamed x1, local copies, waits for them, and re-layouts  1.39 us

commit v1 on v0

--- a/solution.py
+++ b/solution.py
@@ -273,6 +273,306 @@
     each_from(1, experts, left_expert)
 
 
+def relay_kernel(experts, dp, topk, first, slots, pad, bands,
+                 tok_hbm, ids_hbm, gates_hbm, placement_hbm, wg_hbm, wu_hbm, wd_hbm, out,
+                 ids, gates, placement, rows, flat, wg, wu, wd, hid, part_s, part_r, back_s,
+                 l_sem, w_s, w_r, z_s, z_r, d_s, d_r, c_s, c_r, h_s, h_r, p_s, p_r, b_s, b_r):
+    me_e = lax.axis_index("expert")
+    me_j = lax.axis_index("dp")
+    core = lax.rem(me_e, 2)
+    z = lax.div(me_e, 2)
+    chips = experts // 2
+    far = chips - 1
+    own = rows.shape[3]
+    width = tok_hbm.shape[1]
+    half = width // 2
+    both = 2 * own
+    span = dp * both
+    band = width // bands
+
+    def turn(at, q):
+        return q + lax.div(at, chips // 2) * (far - 2 * q)
+
+    def chip_at(k):
+        q = k - 1 + lax.div(k - 1 + chips - turn(z, z), chips)
+        return turn(z, q)
+
+    def seen_from(other):
+        q = turn(other, z)
+        return q + 1 - lax.div(q + chips - turn(other, other), chips)
+
+    low, high = lax.rem(me_j, 2), lax.div(me_j, 2)
+    across = (me_j, high * 2 + (1 - low), (1 - high) * 2 + low, (1 - high) * 2 + (1 - low))
+    sibling = z * 2 + (1 - core)
+
+    def to_dp(src, dst, send, recv, s):
+        return pltpu.make_async_remote_copy(src_ref=src, dst_ref=dst, send_sem=send, recv_sem=recv,
+                                            device_id={"dp": across[s]}, device_id_type=MESH)
+
+    def to_expert(src, dst, send, recv, e):
+        return pltpu.make_async_remote_copy(src_ref=src, dst_ref=dst, send_sem=send, recv_sem=recv,
+                                            device_id={"expert": e}, device_id_type=MESH)
+
+    def edge(b):
+        return 0 if b == 0 else pad + b * band
+
+    def cols(b0, b1):
+        return pl.ds(edge(b0), edge(b1) - edge(b0))
+
+    whole = ((0, bands),)
+    halves = ((0, bands // 2), (bands // 2, bands))
+    single = tuple((b, b + 1) for b in range(bands))
+    z_cuts = halves
+    cuts = tuple(single if k == far else halves if k == far - 1 else whole for k in range(chips))
+
+    barrier = pltpu.get_barrier_semaphore()
+    for s in range(1, dp):
+        pl.semaphore_signal(barrier, inc=1, device_id={"dp": across[s]}, device_id_type=MESH)
+    for d in range(1, experts):
+        pl.semaphore_signal(barrier, inc=1, device_id={"expert": lax.rem(me_e + d, experts)}, device_id_type=MESH)
+
+    mine = rows.at[core, 0, me_j]
+    kept = pl.ds(pl.multiple_of(core * half, 128), half)
+    given = pl.ds(pl.multiple_of((1 - core) * half, 128), half)
+    loads = [pltpu.make_async_copy(a, b, l_sem.at[i]) for i, (a, b) in enumerate((
+        (ids_hbm, ids), (gates_hbm, gates), (placement_hbm, placement),
+        (tok_hbm, mine.at[:, pl.ds(pad, width)]),
+        (wg_hbm, wg), (wu_hbm, wu), (wd_hbm.at[:, kept], wd.at[core])))]
+    for load in loads:
+        load.start()
+    for load in loads[:3]:
+        load.wait()
+
+    lane = lax.broadcasted_iota(jnp.int32, (own, pad), 1)
+    line = lax.broadcasted_iota(jnp.int32, (own, pad), 0)
+    id_f = ids[...].astype(F32)
+    gate_f = gates[...].astype(F32)
+    info = jnp.zeros((own, pad), F32)
+    for t in range(own):
+        for k in range(topk):
+            for at, table in ((k, id_f), (topk + k, gate_f)):
+                here = jnp.where(line == t, lane, -1) == at
+                info = jnp.where(here, jnp.broadcast_to(table[k:k + 1, t:t + 1], (own, pad)), info)
+    rows[core, 0, me_j, :, 0:pad] = info.astype(BF16)
+    loads[3].wait()
+    pl.semaphore_wait(barrier, dp - 1 + experts - 1)
+
+    def over_z(k, i):
+        other = chip_at(k)
+        c = cols(*z_cuts[i])
+        return to_expert(mine.at[:, c], rows.at[core, seen_from(other), me_j, :, c], z_s.at[k, i],
+                         z_r.at[seen_from(other), i], other * 2 + core)
+
+    def from_z(k, i):
+        c = cols(*z_cuts[i])
+        here = rows.at[core, k, me_j, :, c]
+        return to_expert(here, here, z_s.at[k, i], z_r.at[k, i], sibling)
+
+    def over_dp(k, i, s, at):
+        here = rows.at[core, k, at, :, cols(*cuts[k][i])]
+        return to_dp(here, here, d_s.at[k, s, i], d_r.at[k, s, i], s)
+
+    def across_core(k, i, c):
+        here = rows.at[c, k, :, :, cols(*cuts[k][i])]
+        return to_expert(here, here, c_s.at[k, i], c_r.at[k, i], sibling)
+
+    for k in range(1, chips):
+        for i in range(len(z_cuts)):
+            over_z(k, i).start()
+    for s in range(1, dp):
+        over_dp(0, 0, s, me_j).start()
+    lend = to_expert(wd_hbm.at[:, given], wd.at[core], w_s, w_r, sibling)
+    lend.start()
+
+    def pass_on(k):
+        for i, (b0, b1) in enumerate(cuts[k]):
+            for n, (a0, a1) in enumerate(z_cuts):
+                if a0 < b1 and a1 > b0 and a0 >= b0:
+                    from_z(k, n).wait_recv()
+            for s in range(1, dp):
+                over_dp(k, i, s, me_j).start()
+
+    def share(k, i):
+        for s in range(1, dp):
+            over_dp(k, i, s, across[s]).wait_recv()
+        across_core(k, i, core).start()
+
+    def spread(k, i):
+        across_core(k, i, 1 - core).wait_recv()
+        c = cols(*cuts[k][i])
+        at = (k % 2) * span
+        for o in range(2):
+            for j in range(dp):
+                start = at + j * both + o * own
+                flat[k // 2, start:start + own, c] = rows[o, k, j, :, c].astype(F32)
+
+    for k in range(1, chips):
+        pass_on(k)
+    share(0, 0)
+    share(1, 0)
+    spread(0, 0)
+    spread(1, 0)
+
+    contract = (((1,), (1,)), ((), ()))
+    loads[4].wait()
+    loads[5].wait()
+
+    def gate_up(p, b, gate, up):
+        c = pl.ds(b * band, band)
+        x = flat[p, :, pl.ds(pad + b * band, band)].astype(BF16)
+        gate_part = lax.dot_general(x, wg[:, c], contract, preferred_element_type=F32)
+        up_part = lax.dot_general(x, wu[:, c], contract, preferred_element_type=F32)
+        return (gate_part, up_part) if gate is None else (gate + gate_part, up + up_part)
+
+    me_f = me_e.astype(F32)
+    many = 2 * span
+    r = lax.broadcasted_iota(jnp.int32, (many, many), 0)
+    q = lax.broadcasted_iota(jnp.int32, (many, many), 1)
+    same = jnp.where(lax.div(r, span) == lax.div(q, span), lax.rem(lax.div(r, own), 2), 2) == lax.rem(lax.div(q, own), 2)
+    below = jnp.where(same, jnp.where(q < r, 1.0, 0.0), 0.0).astype(BF16)
+    listed = placement[0:1, :].astype(F32)
+    extra = jnp.sum(jnp.where(listed == me_f, float(slots - first), 0.0), axis=1, keepdims=True)
+    limit = float(first) + extra
+
+    def weigh(p):
+        told = flat[p, :, 0:pad]
+        named = jnp.zeros((many, 1), F32)
+        value = jnp.zeros((many, 1), F32)
+        for k in range(topk):
+            hit = told[:, k:k + 1] == me_f
+            named = named + jnp.where(hit, 1.0, 0.0)
+            value = value + jnp.where(hit, told[:, topk + k:topk + k + 1], 0.0)
+        rank = jnp.dot(below, jnp.broadcast_to(named, (many, 128)).astype(BF16), preferred_element_type=F32)[:, 0:1]
+        return jnp.where(rank < limit, value, 0.0)
+
+    def finish(p, gate, up, weight):
+        hid[core, p * many:(p + 1) * many, :] = (gate / (1.0 + jnp.exp(-gate)) * up * weight).astype(BF16)
+
+    gate = up = None
+    todo = [(k, i) for k in range(2, chips) for i in range(len(cuts[k]))]
+    for b in range(bands):
+        gate, up = gate_up(0, b, gate, up)
+        for k, i in todo[b * len(todo) // bands:(b + 1) * len(todo) // bands]:
+            share(k, i)
+    finish(0, gate, up, weigh(0))
+
+    gate = up = None
+    for b in range(bands):
+        for k in range(2, chips):
+            for i, (b0, b1) in enumerate(cuts[k]):
+                if b0 == b:
+                    spread(k, i)
+        gate, up = gate_up(1, b, gate, up)
+    finish(1, gate, up, weigh(1))
+
+    swap = to_expert(hid.at[core], hid.at[core], h_s, h_r, sibling)
+    swap.start()
+    loads[6].wait()
+    to_expert(wd.at[1 - core], wd.at[1 - core], w_s, w_r, sibling).wait_recv()
+    to_expert(hid.at[1 - core], hid.at[1 - core], h_s, h_r, sibling).wait_recv()
+    piece = half // bands
+    for b in range(bands):
+        c = pl.ds(b * piece, piece)
+        total = jnp.dot(hid[0], wd[0, :, c], preferred_element_type=F32)
+        total = total + jnp.dot(hid[1], wd[1, :, c], preferred_element_type=F32)
+        part_s[:, :, c] = total.reshape(chips * dp, both, piece).astype(BF16)
+
+    def over_part(k, s):
+        return to_dp(part_s.at[k * dp + across[s]], part_r.at[k, s], p_s.at[k, s], p_r.at[k, s], s)
+
+    for k in reversed(range(chips)):
+        for s in reversed(range(1, dp)):
+            over_part(k, s).start()
+
+    def over_back(k, o):
+        e = sibling if k == 0 else chip_at(k) * 2 + o
+        return to_expert(back_s.at[k, o], out.at[z, :, kept], b_s.at[k, o], b_r.at[z, core], e)
+
+    for k in reversed(range(chips)):
+        value = part_s[k * dp + me_j].astype(F32)
+        for s in range(1, dp):
+            over_part(k, s).wait_recv()
+            value = value + part_r[k, s].astype(F32)
+        for o in range(2):
+            back_s[k, o] = value[o * own:(o + 1) * own, :].astype(BF16)
+        if k > 0:
+            for o in range(2):
+                over_back(k, o).start()
+    give = to_expert(back_s.at[0, 1 - core], out.at[z, :, kept], b_s.at[0, 0], b_r.at[z, core], sibling)
+    give.start()
+    keep = pltpu.make_async_copy(back_s.at[0, core], out.at[z, :, kept], b_s.at[0, 1])
+    keep.start()
+
+    keep.wait()
+    to_expert(back_s.at[0, core], out.at[z, :, given], b_s.at[0, 0], b_r.at[z, 1 - core], sibling).wait_recv()
+    for k in range(1, chips):
+        other = chip_at(k)
+        for o in range(2):
+            to_expert(back_s.at[k, o], out.at[other, :, pl.ds(o * half, half)], b_s.at[k, o], b_r.at[other, o],
+                      sibling).wait_recv()
+
+    lend.wait_send()
+    swap.wait_send()
+    give.wait_send()
+    for k in range(chips):
+        for i in range(len(z_cuts)):
+            if k > 0:
+                over_z(k, i).wait_send()
+        for i in range(len(cuts[k])):
+            for s in range(1, dp):
+                over_dp(k, i, s, me_j).wait_send()
+            across_core(k, i, core).wait_send()
+        for s in range(1, dp):
+            over_part(k, s).wait_send()
+        if k > 0:
+            for o in range(2):
+                over_back(k, o).wait_send()
+
+
+def relayed(tokens, expert_ids, gate_weights, placement, w_gate, w_up, w_down, experts, dp, first, slots):
+    own, width = tokens.shape
+    topk = expert_ids.shape[1]
+    units = w_gate.shape[1]
+    chips = experts // 2
+    bands = 4
+    pad = 128
+    half = width // 2
+    hbm = pl.BlockSpec(memory_space=pl.ANY)
+    dma = pltpu.SemaphoreType.DMA
+    parts = pl.pallas_call(
+        functools.partial(relay_kernel, experts, dp, topk, first, slots, pad, bands),
+        out_shape=jax.ShapeDtypeStruct((chips, own, width), BF16),
+        in_specs=[hbm] * 7,
+        out_specs=hbm,
+        scratch_shapes=[
+            pltpu.VMEM((topk, own), jnp.int32),
+            pltpu.VMEM((topk, own), BF16),
+            pltpu.VMEM(placement.shape, jnp.int32),
+            pltpu.VMEM((2, chips, dp, own, pad + width), BF16),
+            pltpu.VMEM((chips // 2, 4 * dp * own, pad + width), F32),
+            pltpu.VMEM((units, width), BF16),
+            pltpu.VMEM((units, width), BF16),
+            pltpu.VMEM((2, units, half), BF16),
+            pltpu.VMEM((2, experts * dp * own, units), BF16),
+            pltpu.VMEM((chips * dp, 2 * own, half), BF16),
+            pltpu.VMEM((chips, dp, 2 * own, half), BF16),
+            pltpu.VMEM((chips, 2, own, half), BF16),
+            dma((7,)),
+            dma, dma,
+            dma((chips, 2)), dma((chips, 2)),
+            dma((chips, dp, bands)), dma((chips, dp, bands)),
+            dma((chips, bands)), dma((chips, bands)),
+            dma, dma,
+            dma((chips, dp)), dma((chips, dp)),
+            dma((chips, 2)), dma((chips, 2)),
+        ],
+        compiler_params=pltpu.CompilerParams(
+            collective_id=1, has_side_effects=True, vmem_limit_bytes=56 << 20
+        ),
+    )(tokens, expert_ids.T, gate_weights.T, placement, w_gate[0], w_up[0], w_down[0])
+    return jnp.sum(parts.astype(F32), axis=0).astype(BF16)
+
+
 def body(tokens, expert_ids, gate_weights, placement, w_gate, w_up, w_down):
     experts = lax.axis_size("expert")
     dp = lax.axis_size("dp")
@@ -281,6 +581,8 @@
     group = own * dp
     first = max(2, group * topk // experts)
     slots = first + max(1, first // 2)
+    if dp == 4 and experts == 8 and own == 4 and width % 1024 == 0:
+        return relayed(tokens, expert_ids, gate_weights, placement, w_gate, w_up, w_down, experts, dp, first, slots)
     padded = -(-slots // 8) * 8
     lanes = -(-group * topk // 128) * 128
     block = width // dp

time: 36.4 us -> 34.8 us (0.956)
  Pallas kernels: 34.9 us -> 33 us
  other arithmetic: 0 us -> 1.6 us
  local copies, waits for them, and re-layouts: 1.39 us -> 0 us
    pallas_call x1, Pallas kernels: 34.9 us -> 33 us  [relayed(): pl.pallas_call(functools.partial(relay_kernel, experts, dp, topk, first,...]
    reduce_sum x0 -> x1, other arithmetic: none -> 1.6 us  [relayed(): return jnp.sum(parts.astype(F32), axis=0).astype(BF16)]
    unnamed x1 -> x0, local copies, waits for them, and re-layouts: 1.39 us -> none
where the time goes in v1:
time: 34.8 us; the launch traced here: 34.6 us
  Pallas kernels  33 us (95%)
  other arithmetic  1.6 us (5%)
    pallas_call x1, Pallas kernels, relayed(): pl.pallas_call(functools.partial(relay_kernel, experts, dp, topk, first,...  33 us
    reduce_sum x1, other arithmetic, relayed(): return jnp.sum(parts.astype(F32), axis=0).astype(BF16)  1.6 us

profile of v1, /device:TPU:0, one launch (start us, length us, event | category | flops | bytes accessed | tf_op | source)
XLA Modules:
  0.0 34.6 jit_solution(11707606102276882802)
XLA Ops:
  0.0 33.0 %shard_map.73 = bf16[4,4,4096]{2,1,0:T(4,128)(2,1)} custom-call(bf16[4,4096]{1,0:T(4,128)(2,1)} %tok_hbm.1, s32[2,4]{1,0:T(2,128)} %bitcast.8, bf16[2,4]{1,0:T(2,128)(2,1)} %bitcast.9, s32[2,2]{1,0:T(2,128)} %placement_hbm.1, bf16[384,4096]{1,0:T(8,128)(2,1)} %bitcast.5, bf16[384,4096]{1,0:T(8,128)(2,1)} %bitcast.6, bf16[384,4096]{1,0:T(8,128)(2,1)} %bitcast.7), custom_call_target="tpu_custom_call" | custom-call | tf_op jit(solution)/shard_map/pallas_call | solution.py:542
  33.0 1.6 %reduce_sum.12 = bf16[4,4096]{1,0:T(4,128)(2,1)} reduce(bf16[4,4,4096]{2,1,0:T(4,128)(2,1)} %shard_map.73, bf16[]{:T(256)} %constant.2.clone.1), dimensions={0}, to_apply=%region_0.0 | reduce | flops 49152 | bytes 163842 | tf_op jit(solution)/shard_map/reduce_sum | solution.py:573

commit v2 on v1

--- a/solution.py
+++ b/solution.py
@@ -276,7 +276,7 @@
 def relay_kernel(experts, dp, topk, first, slots, pad, bands,
                  tok_hbm, ids_hbm, gates_hbm, placement_hbm, wg_hbm, wu_hbm, wd_hbm, out,
                  ids, gates, placement, rows, flat, wg, wu, wd, hid, part_s, part_r, back_s,
-                 l_sem, w_s, w_r, z_s, z_r, d_s, d_r, c_s, c_r, h_s, h_r, p_s, p_r, b_s, b_r):
+                 ready_e, ready_d, l_sem, w_s, w_r, z_s, z_r, d_s, d_r, c_s, c_r, h_s, h_r, p_s, p_r, b_s, b_r):
     me_e = lax.axis_index("expert")
     me_j = lax.axis_index("dp")
     core = lax.rem(me_e, 2)
@@ -326,10 +326,26 @@
     cuts = tuple(single if k == far else halves if k == far - 1 else whole for k in range(chips))
 
     barrier = pltpu.get_barrier_semaphore()
-    for s in range(1, dp):
-        pl.semaphore_signal(barrier, inc=1, device_id={"dp": across[s]}, device_id_type=MESH)
-    for d in range(1, experts):
-        pl.semaphore_signal(barrier, inc=1, device_id={"expert": lax.rem(me_e + d, experts)}, device_id_type=MESH)
+
+    def tell(sem, axis, to):
+        pl.semaphore_signal(sem, inc=1, device_id={axis: to}, device_id_type=MESH)
+
+    tell(barrier, "expert", sibling)
+    for s in range(1, dp):
+        pl.when(across[s] > me_j)(functools.partial(tell, barrier, "dp", across[s]))
+    for q in range(1, chips):
+        for o in range(2):
+            pl.when(q > z)(functools.partial(tell, barrier, "expert", q * 2 + o))
+
+    def meet_dp(s):
+        @pl.when(across[s] > me_j)
+        def _():
+            pl.semaphore_wait(ready_d.at[s], 1)
+
+    def meet_chip(q, o):
+        @pl.when(q > z)
+        def _():
+            pl.semaphore_wait(ready_e.at[q, o], 1)
 
     mine = rows.at[core, 0, me_j]
     kept = pl.ds(pl.multiple_of(core * half, 128), half)
@@ -355,12 +371,21 @@
                 info = jnp.where(here, jnp.broadcast_to(table[k:k + 1, t:t + 1], (own, pad)), info)
     rows[core, 0, me_j, :, 0:pad] = info.astype(BF16)
     loads[3].wait()
-    pl.semaphore_wait(barrier, dp - 1 + experts - 1)
-
-    def over_z(k, i):
-        other = chip_at(k)
+    pl.semaphore_wait(barrier, 1 + 2 * z + me_j)
+    for s in range(1, dp):
+        pl.when(across[s] < me_j)(functools.partial(tell, ready_d.at[s], "dp", across[s]))
+    for q in range(chips - 1):
+        for o in range(2):
+            pl.when(q < z)(functools.partial(tell, ready_e.at[z, core], "expert", q * 2 + o))
+
+    def sent_to(n):
+        before = lax.div(z - n - 1 + chips, chips)
+        return before * (z - 1 - n) + (1 - before) * (n + 1)
+
+    def over_z(n, i):
+        other = sent_to(n)
         c = cols(*z_cuts[i])
-        return to_expert(mine.at[:, c], rows.at[core, seen_from(other), me_j, :, c], z_s.at[k, i],
+        return to_expert(mine.at[:, c], rows.at[core, seen_from(other), me_j, :, c], z_s.at[n, i],
                          z_r.at[seen_from(other), i], other * 2 + core)
 
     def from_z(k, i):
@@ -376,11 +401,13 @@
         here = rows.at[c, k, :, :, cols(*cuts[k][i])]
         return to_expert(here, here, c_s.at[k, i], c_r.at[k, i], sibling)
 
-    for k in range(1, chips):
+    for s in range(1, dp):
+        meet_dp(s)
+        over_dp(0, 0, s, me_j).start()
+    for n in range(chips - 1):
+        meet_chip(sent_to(n), core)
         for i in range(len(z_cuts)):
-            over_z(k, i).start()
-    for s in range(1, dp):
-        over_dp(0, 0, s, me_j).start()
+            over_z(n, i).start()
     lend = to_expert(wd_hbm.at[:, given], wd.at[core], w_s, w_r, sibling)
     lend.start()
 
@@ -406,11 +433,12 @@
                 start = at + j * both + o * own
                 flat[k // 2, start:start + own, c] = rows[o, k, j, :, c].astype(F32)
 
-    for k in range(1, chips):
+    pass_on(1)
+    share(0, 0)
+    for k in range(2, chips):
         pass_on(k)
-    share(0, 0)
+    spread(0, 0)
     share(1, 0)
-    spread(0, 0)
     spread(1, 0)
 
     contract = (((1,), (1,)), ((), ()))
@@ -445,8 +473,30 @@
         rank = jnp.dot(below, jnp.broadcast_to(named, (many, 128)).astype(BF16), preferred_element_type=F32)[:, 0:1]
         return jnp.where(rank < limit, value, 0.0)
 
+    def swap(p, at):
+        here = hid.at[at, p]
+        return to_expert(here, here, h_s.at[p], h_r.at[p], sibling)
+
     def finish(p, gate, up, weight):
-        hid[core, p * many:(p + 1) * many, :] = (gate / (1.0 + jnp.exp(-gate)) * up * weight).astype(BF16)
+        hid[core, p] = (gate / (1.0 + jnp.exp(-gate)) * up * weight).astype(BF16)
+        swap(p, core).start()
+
+    def over_part(k, s):
+        return to_dp(part_s.at[k * dp + across[s]], part_r.at[k, s], p_s.at[k, s], p_r.at[k, s], s)
+
+    piece = half // bands
+
+    def down(p):
+        swap(p, 1 - core).wait_recv()
+        for b in range(bands):
+            c = pl.ds(b * piece, piece)
+            total = jnp.dot(hid[0, p], wd[0, :, c], preferred_element_type=F32)
+            total = total + jnp.dot(hid[1, p], wd[1, :, c], preferred_element_type=F32)
+            part_s[2 * p * dp:2 * (p + 1) * dp, :, c] = total.reshape(2 * dp, both, piece).astype(BF16)
+
+    def send_part(k):
+        for s in reversed(range(1, dp)):
+            over_part(k, s).start()
 
     gate = up = None
     todo = [(k, i) for k in range(2, chips) for i in range(len(cuts[k]))]
@@ -465,30 +515,21 @@
         gate, up = gate_up(1, b, gate, up)
     finish(1, gate, up, weigh(1))
 
-    swap = to_expert(hid.at[core], hid.at[core], h_s, h_r, sibling)
-    swap.start()
     loads[6].wait()
     to_expert(wd.at[1 - core], wd.at[1 - core], w_s, w_r, sibling).wait_recv()
-    to_expert(hid.at[1 - core], hid.at[1 - core], h_s, h_r, sibling).wait_recv()
-    piece = half // bands
-    for b in range(bands):
-        c = pl.ds(b * piece, piece)
-        total = jnp.dot(hid[0], wd[0, :, c], preferred_element_type=F32)
-        total = total + jnp.dot(hid[1], wd[1, :, c], preferred_element_type=F32)
-        part_s[:, :, c] = total.reshape(chips * dp, both, piece).astype(BF16)
-
-    def over_part(k, s):
-        return to_dp(part_s.at[k * dp + across[s]], part_r.at[k, s], p_s.at[k, s], p_r.at[k, s], s)
-
-    for k in reversed(range(chips)):
-        for s in reversed(range(1, dp)):
-            over_part(k, s).start()
+    down(0)
+    send_part(1)
+    down(1)
+    for k in (3, 2, 0):
+        send_part(k)
+    for k in range(1, chips):
+        meet_chip(chip_at(k), 1 - core)
 
     def over_back(k, o):
         e = sibling if k == 0 else chip_at(k) * 2 + o
         return to_expert(back_s.at[k, o], out.at[z, :, kept], b_s.at[k, o], b_r.at[z, core], e)
 
-    for k in reversed(range(chips)):
+    for k in (1, 3, 2, 0):
         value = part_s[k * dp + me_j].astype(F32)
         for s in range(1, dp):
             over_part(k, s).wait_recv()
@@ -512,12 +553,13 @@
                       sibling).wait_recv()
 
     lend.wait_send()
-    swap.wait_send()
+    for p in range(2):
+        swap(p, core).wait_send()
     give.wait_send()
     for k in range(chips):
         for i in range(len(z_cuts)):
             if k > 0:
-                over_z(k, i).wait_send()
+                over_z(k - 1, i).wait_send()
         for i in range(len(cuts[k])):
             for s in range(1, dp):
                 over_dp(k, i, s, me_j).wait_send()
@@ -553,16 +595,17 @@
             pltpu.VMEM((units, width), BF16),
             pltpu.VMEM((units, width), BF16),
             pltpu.VMEM((2, units, half), BF16),
-            pltpu.VMEM((2, experts * dp * own, units), BF16),
+            pltpu.VMEM((2, 2, 4 * dp * own, units), BF16),
             pltpu.VMEM((chips * dp, 2 * own, half), BF16),
             pltpu.VMEM((chips, dp, 2 * own, half), BF16),
             pltpu.VMEM((chips, 2, own, half), BF16),
+            pltpu.SemaphoreType.REGULAR((chips, 2)), pltpu.SemaphoreType.REGULAR((dp,)),
             dma((7,)),
             dma, dma,
             dma((chips, 2)), dma((chips, 2)),
             dma((chips, dp, bands)), dma((chips, dp, bands)),
             dma((chips, bands)), dma((chips, bands)),
-            dma, dma,
+            dma((2,)), dma((2,)),
             dma((chips, dp)), dma((chips, dp)),
             dma((chips, 2)), dma((chips, 2)),
         ],

time: 34.8 us -> 33.3 us (0.957)
  Pallas kernels: 33 us -> 31.5 us
    pallas_call x1, Pallas kernels: 33 us -> 31.5 us  [relayed(): pl.pallas_call(functools.partial(relay_kernel, experts, dp, topk, first,...]
where the time goes in v2:
time: 33.3 us; the launch traced here: 33.1 us
  Pallas kernels  31.5 us (95%)
  other arithmetic  1.6 us (5%)
    pallas_call x1, Pallas kernels, relayed(): pl.pallas_call(functools.partial(relay_kernel, experts, dp, topk, first,...  31.5 us
    reduce_sum x1, other arithmetic, relayed(): return jnp.sum(parts.astype(F32), axis=0).astype(BF16)  1.6 us

profile of v2, /device:TPU:0, one launch (start us, length us, event | category | flops | bytes accessed | tf_op | source)
XLA Modules:
  0.0 33.1 jit_solution(4677435249531639627)
XLA Ops:
  0.0 31.5 %shard_map.73 = bf16[4,4,4096]{2,1,0:T(4,128)(2,1)} custom-call(bf16[4,4096]{1,0:T(4,128)(2,1)} %tok_hbm.1, s32[2,4]{1,0:T(2,128)} %bitcast.8, bf16[2,4]{1,0:T(2,128)(2,1)} %bitcast.9, s32[2,2]{1,0:T(2,128)} %placement_hbm.1, bf16[384,4096]{1,0:T(8,128)(2,1)} %bitcast.5, bf16[384,4096]{1,0:T(8,128)(2,1)} %bitcast.6, bf16[384,4096]{1,0:T(8,128)(2,1)} %bitcast.7), custom_call_target="tpu_custom_call" | custom-call | tf_op jit(solution)/shard_map/pallas_call | solution.py:584
  31.5 1.6 %reduce_sum.12 = bf16[4,4096]{1,0:T(4,128)(2,1)} reduce(bf16[4,4,4096]{2,1,0:T(4,128)(2,1)} %shard_map.73, bf16[]{:T(256)} %constant.2.clone.1), dimensions={0}, to_apply=%region_0.0 | reduce | flops 49152 | bytes 163842 | tf_op jit(solution)/shard_map/reduce_sum | solution.py:616

commit v3 on v0

--- a/solution.py
+++ b/solution.py
@@ -273,6 +273,335 @@
     each_from(1, experts, left_expert)
 
 
+def relay_kernel(experts, dp, topk, first, slots, pad, bands, cuts,
+                 tok_hbm, ids_hbm, gates_hbm, placement_hbm, wg_hbm, wu_hbm, wd_hbm, out,
+                 ids, gates, placement, rows, flat, wgu, wd, acc, hid, part_s, part_r, back_s,
+                 ready_e, ready_d, l_sem, w_sem, z_s, z_r, d_s, d_r, f_s, c_s, c_r, h_sem, p_s, p_r, b_s, b_r):
+    me_e = lax.axis_index("expert")
+    me_j = lax.axis_index("dp")
+    core = lax.rem(me_e, 2)
+    z = lax.div(me_e, 2)
+    chips = experts // 2
+    far = chips - 1
+    own = rows.shape[3]
+    width = tok_hbm.shape[1]
+    units = wg_hbm.shape[0]
+    half = width // 2
+    both = 2 * own
+    span = dp * both
+    many = chips * span
+    band = width // bands
+
+    def turn(at, q):
+        return q + lax.div(at, chips // 2) * (far - 2 * q)
+
+    def chip_at(k):
+        q = k - 1 + lax.div(k - 1 + chips - turn(z, z), chips)
+        return turn(z, q)
+
+    def seen_from(other):
+        q = turn(other, z)
+        return q + 1 - lax.div(q + chips - turn(other, other), chips)
+
+    def sent_to(n):
+        before = lax.div(z - n - 1 + chips, chips)
+        return before * (z - 1 - n) + (1 - before) * (n + 1)
+
+    low, high = lax.rem(me_j, 2), lax.div(me_j, 2)
+    across = (me_j, high * 2 + (1 - low), (1 - high) * 2 + low, (1 - high) * 2 + (1 - low))
+    sibling = z * 2 + (1 - core)
+
+    def to_dp(src, dst, send, recv, s):
+        return pltpu.make_async_remote_copy(src_ref=src, dst_ref=dst, send_sem=send, recv_sem=recv,
+                                            device_id={"dp": across[s]}, device_id_type=MESH)
+
+    def to_expert(src, dst, send, recv, e):
+        return pltpu.make_async_remote_copy(src_ref=src, dst_ref=dst, send_sem=send, recv_sem=recv,
+                                            device_id={"expert": e}, device_id_type=MESH)
+
+    def landed(ref, sem):
+        to_expert(ref, ref, sem, sem, sibling).wait_recv()
+
+    def left(ref, sem):
+        to_expert(ref, ref, sem, sem, sibling).wait_send()
+
+    def edge(b):
+        return 0 if b == 0 else pad + b * band
+
+    def cols(b0, b1):
+        return pl.ds(edge(b0), edge(b1) - edge(b0))
+
+    z_cuts = ((0, bands // 2), (bands // 2, bands))
+    at_cut = {}
+    for k in range(chips):
+        for i in range(len(cuts[k])):
+            at_cut[k, i] = len(at_cut)
+
+    barrier = pltpu.get_barrier_semaphore()
+
+    def tell(sem, axis, to):
+        pl.semaphore_signal(sem, inc=1, device_id={axis: to}, device_id_type=MESH)
+
+    tell(barrier, "expert", sibling)
+    for s in range(1, dp):
+        pl.when(across[s] > me_j)(functools.partial(tell, barrier, "dp", across[s]))
+    for q in range(1, chips):
+        for o in range(2):
+            pl.when(q > z)(functools.partial(tell, barrier, "expert", q * 2 + o))
+
+    def meet_dp(s):
+        @pl.when(across[s] > me_j)
+        def _():
+            pl.semaphore_wait(ready_d.at[s - 1], 1)
+
+    def meet_chip(q, o):
+        @pl.when(q > z)
+        def _():
+            pl.semaphore_wait(ready_e.at[q - 1, o], 1)
+
+    mine = rows.at[core, 0, me_j]
+    kept = pl.ds(pl.multiple_of(core * half, 128), half)
+    given = pl.ds(pl.multiple_of((1 - core) * half, 128), half)
+    loads = [pltpu.make_async_copy(a, b, l_sem.at[i]) for i, (a, b) in enumerate((
+        (ids_hbm, ids), (gates_hbm, gates), (placement_hbm, placement),
+        (tok_hbm, mine.at[:, pl.ds(pad, width)]),
+        (wg_hbm, wgu.at[pl.ds(0, units)]), (wu_hbm, wgu.at[pl.ds(units, units)]),
+        (wd_hbm.at[:, kept], wd.at[core])))]
+    for load in loads:
+        load.start()
+    pl.semaphore_wait(barrier, 1 + 2 * z + me_j)
+    for q in range(chips - 1):
+        for o in range(2):
+            pl.when(q < z)(functools.partial(tell, ready_e.at[z - 1, core], "expert", q * 2 + o))
+    for s in range(1, dp):
+        pl.when(across[s] < me_j)(functools.partial(tell, ready_d.at[s - 1], "dp", across[s]))
+
+    for load in loads[:3]:
+        load.wait()
+    lane = lax.broadcasted_iota(jnp.int32, (own, pad), 1)
+    line = lax.broadcasted_iota(jnp.int32, (own, pad), 0)
+    id_f = ids[...].astype(F32)
+    gate_f = gates[...].astype(F32)
+    info = jnp.zeros((own, pad), F32)
+    for t in range(own):
+        for k in range(topk):
+            for at, table in ((k, id_f), (topk + k, gate_f)):
+                here = jnp.where(line == t, lane, -1) == at
+                info = jnp.where(here, jnp.broadcast_to(table[k:k + 1, t:t + 1], (own, pad)), info)
+    rows[core, 0, me_j, :, 0:pad] = info.astype(BF16)
+    loads[3].wait()
+
+    def over_dp(k, i, s, at):
+        here = rows.at[core, k, at, :, cols(*cuts[k][i])]
+        return to_dp(here, here, d_s.at[k], d_r.at[at_cut[k, i]], s)
+
+    for s in range(1, dp):
+        meet_dp(s)
+        over_dp(0, 0, s, me_j).start()
+    for n in range(chips - 1):
+        other = sent_to(n)
+        k = seen_from(other)
+        meet_chip(other, core)
+        for i in range(len(z_cuts)):
+            c = cols(*z_cuts[i])
+            to_expert(mine.at[:, c], rows.at[core, k, me_j, :, c], z_s, z_r.at[k - 1, i], other * 2 + core).start()
+    lend = to_expert(wd_hbm.at[:, given], wd.at[core], w_sem.at[0], w_sem.at[1], sibling)
+    lend.start()
+
+    def pass_on(k):
+        for i, (b0, b1) in enumerate(cuts[k]):
+            for n, (a0, a1) in enumerate(z_cuts):
+                if b0 <= a0 < b1:
+                    landed(rows.at[core, k, me_j, :, cols(a0, a1)], z_r.at[k - 1, n])
+
+            def onward():
+                for s in range(1, dp):
+                    over_dp(k, i, s, me_j).start()
+
+            if k == far:
+                pl.when(z != far)(onward)
+            else:
+                onward()
+
+    def share(k, i):
+        c = cols(*cuts[k][i])
+        landed(rows.at[core, k, pl.ds(0, dp - 1), :, c], d_r.at[at_cut[k, i]])
+        here = rows.at[core, k, :, :, c]
+        to_expert(here, here, c_s.at[k], c_r.at[at_cut[k, i]], sibling).start()
+
+    def spread(k, i):
+        c = cols(*cuts[k][i])
+        landed(rows.at[1 - core, k, :, :, c], c_r.at[at_cut[k, i]])
+        for o in range(2):
+            for j in range(dp):
+                start = k * span + j * both + o * own
+                flat[start:start + own, c] = rows[o, k, j, :, c].astype(F32)
+
+    pass_on(1)
+    share(0, 0)
+
+    @pl.when(z == 0)
+    def _():
+        for i in range(len(cuts[far])):
+            c = cols(*cuts[far][i])
+            for s in range(1, dp):
+                to_expert(rows.at[core, 0, across[s], :, c], rows.at[core, far, across[s], :, c], f_s,
+                          d_r.at[at_cut[far, i]], far * 2 + core).start()
+
+    for k in range(2, chips):
+        pass_on(k)
+    spread(0, 0)
+    for k in range(1, chips):
+        for i in range(len(cuts[k])):
+            share(k, i)
+        if k > 1:
+            for i in range(len(cuts[k - 1])):
+                spread(k - 1, i)
+
+    contract = (((1,), (1,)), ((), ()))
+    loads[4].wait()
+    loads[5].wait()
+    me_f = me_e.astype(F32)
+    weight = None
+    for b in range(bands):
+        for i, (b0, b1) in enumerate(cuts[far]):
+            if b0 == b:
+                spread(far, i)
+        x = flat[:, pl.ds(pad + b * band, band)].astype(BF16)
+        total = lax.dot_general(x, wgu[:, pl.ds(b * band, band)], contract, preferred_element_type=F32)
+        if b == 0:
+            r = lax.broadcasted_iota(jnp.int32, (many, many), 0)
+            q = lax.broadcasted_iota(jnp.int32, (many, many), 1)
+            of_r = jnp.where(lax.div(r, span) == lax.div(q, span), lax.rem(lax.div(r, own), 2), 2)
+            same = of_r == lax.rem(lax.div(q, own), 2)
+            below = jnp.where(same, jnp.where(q < r, 1.0, 0.0), 0.0).astype(BF16)
+            listed = placement[0:1, :].astype(F32)
+            extra = jnp.sum(jnp.where(listed == me_f, float(slots - first), 0.0), axis=1, keepdims=True)
+            told = flat[:, 0:pad]
+            named = jnp.zeros((many, 1), F32)
+            value = jnp.zeros((many, 1), F32)
+            for k in range(topk):
+                hit = told[:, k:k + 1] == me_f
+                named = named + jnp.where(hit, 1.0, 0.0)
+                value = value + jnp.where(hit, told[:, topk + k:topk + k + 1], 0.0)
+            rank = jnp.dot(below, jnp.broadcast_to(named, (many, 128)).astype(BF16), preferred_element_type=F32)[:, 0:1]
+            weight = jnp.where(rank < float(first) + extra, value, 0.0)
+            acc[...] = total
+        elif b < bands - 1:
+            acc[...] += total
+        else:
+            total = acc[...] + total
+            gate, up = total[:, :units], total[:, units:]
+            hid[core] = (gate / (1.0 + jnp.exp(-gate)) * up * weight).astype(BF16)
+
+    swap = to_expert(hid.at[core], hid.at[core], h_sem.at[0], h_sem.at[1], sibling)
+    swap.start()
+    loads[6].wait()
+    landed(wd.at[1 - core], w_sem.at[1])
+    landed(hid.at[1 - core], h_sem.at[1])
+
+    def send_part(k, c):
+        for s in reversed(range(1, dp)):
+            to_dp(part_s.at[k * dp + across[s], :, c], part_r.at[k, s - 1, :, c], p_s.at[k], p_r.at[k], s).start()
+
+    piece = half // bands
+    for b in range(bands):
+        c = pl.ds(b * piece, piece)
+        total = jnp.dot(hid[0], wd[0, :, c], preferred_element_type=F32)
+        total = total + jnp.dot(hid[1], wd[1, :, c], preferred_element_type=F32)
+        part_s[:, :, c] = total.reshape(chips * dp, both, piece).astype(BF16)
+        send_part(far, c)
+    for k in reversed(range(far)):
+        send_part(k, pl.ds(0, half))
+    for k in range(1, chips):
+        meet_chip(chip_at(k), 1 - core)
+
+    for k in reversed(range(chips)):
+        value = part_s[k * dp + me_j].astype(F32)
+        landed(part_r.at[k], p_r.at[k])
+        for s in range(dp - 1):
+            value = value + part_r[k, s].astype(F32)
+        for o in range(2):
+            back_s[k, o] = value[o * own:(o + 1) * own, :].astype(BF16)
+        if k > 0:
+            for o in range(2):
+                to_expert(back_s.at[k, o], out.at[z, :, kept], b_s.at[0], b_r.at[0], chip_at(k) * 2 + o).start()
+    give = to_expert(back_s.at[0, 1 - core], out.at[z, :, kept], b_s.at[1], b_r.at[1], sibling)
+    give.start()
+    keep = pltpu.make_async_copy(back_s.at[0, core], out.at[z, :, kept], b_s.at[2])
+    keep.start()
+
+    lend.wait_send()
+    swap.wait_send()
+    left(rows.at[core, 0, pl.ds(0, chips - 1)], z_s)
+    for k in range(chips):
+        here = rows.at[core, k, pl.ds(0, dp - 1)]
+        if k == far:
+            pl.when(z != far)(functools.partial(left, here, d_s.at[k]))
+            pl.when(z == 0)(functools.partial(left, here, f_s))
+        else:
+            left(here, d_s.at[k])
+        left(rows.at[core, k], c_s.at[k])
+        left(part_r.at[k], p_s.at[k])
+    keep.wait()
+    give.wait_send()
+    left(out.at[pl.ds(0, chips - 1)], b_s.at[0])
+    landed(out.at[z, :, given], b_r.at[1])
+    landed(out.at[pl.ds(0, chips - 1)], b_r.at[0])
+
+
+def relayed(tokens, expert_ids, gate_weights, placement, w_gate, w_up, w_down, experts, dp, first, slots):
+    own, width = tokens.shape
+    topk = expert_ids.shape[1]
+    units = w_gate.shape[1]
+    chips = experts // 2
+    bands = 4
+    pad = 128
+    half = width // 2
+    many = experts * dp * own
+    whole = ((0, bands),)
+    halves = ((0, bands // 2), (bands // 2, bands))
+    single = tuple((b, b + 1) for b in range(bands))
+    cuts = tuple(single if k == chips - 1 else halves if k == chips - 2 else whole for k in range(chips))
+    parts_of = sum(len(c) for c in cuts)
+    hbm = pl.BlockSpec(memory_space=pl.ANY)
+    dma = pltpu.SemaphoreType.DMA
+    parts = pl.pallas_call(
+        functools.partial(relay_kernel, experts, dp, topk, first, slots, pad, bands, cuts),
+        out_shape=pltpu.VMEM((chips, own, width), BF16),
+        in_specs=[hbm] * 7,
+        out_specs=pl.BlockSpec(memory_space=pltpu.VMEM),
+        scratch_shapes=[
+            pltpu.VMEM((topk, own), jnp.int32),
+            pltpu.VMEM((topk, own), BF16),
+            pltpu.VMEM(placement.shape, jnp.int32),
+            pltpu.VMEM((2, chips, dp, own, pad + width), BF16),
+            pltpu.VMEM((many, pad + width), F32),
+            pltpu.VMEM((2 * units, width), BF16),
+            pltpu.VMEM((2, units, half), BF16),
+            pltpu.VMEM((many, 2 * units), F32),
+            pltpu.VMEM((2, many, units), BF16),
+            pltpu.VMEM((chips * dp, 2 * own, half), BF16),
+            pltpu.VMEM((chips, dp - 1, 2 * own, half), BF16),
+            pltpu.VMEM((chips, 2, own, half), BF16),
+            pltpu.SemaphoreType.REGULAR((chips - 1, 2)), pltpu.SemaphoreType.REGULAR((dp - 1,)),
+            dma((7,)),
+            dma((2,)),
+            dma, dma((chips - 1, 2)),
+            dma((chips,)), dma((parts_of,)),
+            dma,
+            dma((chips,)), dma((parts_of,)),
+            dma((2,)),
+            dma((chips,)), dma((chips,)),
+            dma((3,)), dma((2,)),
+        ],
+        compiler_params=pltpu.CompilerParams(
+            collective_id=1, has_side_effects=True, vmem_limit_bytes=56 << 20
+        ),
+    )(tokens, expert_ids.T, gate_weights.T, placement, w_gate[0], w_up[0], w_down[0])
+    return jnp.sum(parts.astype(F32), axis=0).astype(BF16)
+
+
 def body(tokens, expert_ids, gate_weights, placement, w_gate, w_up, w_down):
     experts = lax.axis_size("expert")
     dp = lax.axis_size("dp")
@@ -281,6 +610,8 @@
     group = own * dp
     first = max(2, group * topk // experts)
     slots = first + max(1, first // 2)
+    if dp == 4 and experts == 8 and own == 4 and width % 1024 == 0:
+        return relayed(tokens, expert_ids, gate_weights, placement, w_gate, w_up, w_down, experts, dp, first, slots)
     padded = -(-slots // 8) * 8
     lanes = -(-group * topk // 128) * 128
     block = width // dp

time: 36.4 us -> 30.5 us (0.84)
  Pallas kernels: 34.9 us -> 29.6 us
  local copies, waits for them, and re-layouts: 1.39 us -> 0 us
  other arithmetic: 0 us -> 0.68 us
    pallas_call x1, Pallas kernels: 34.9 us -> 29.6 us  [relayed(): pl.pallas_call(functools.partial(relay_kernel, experts, dp, topk, first,...]
    unnamed x1 -> x0, local copies, waits for them, and re-layouts: 1.39 us -> none
    reduce_sum x0 -> x1, other arithmetic: none -> 0.68 us  [relayed(): return jnp.sum(parts.astype(F32), axis=0).astype(BF16)]
where the time goes in v3:
time: 30.5 us; the launch traced here: 30.3 us
  Pallas kernels  29.6 us (97%)
  other arithmetic  0.68 us (2%)
    pallas_call x1, Pallas kernels, relayed(): pl.pallas_call(functools.partial(relay_kernel, experts, dp, topk, first,...  29.6 us
    reduce_sum x1, other arithmetic, relayed(): return jnp.sum(parts.astype(F32), axis=0).astype(BF16)  0.68 us

profile of v3, /device:TPU:0, one launch (start us, length us, event | category | flops | bytes accessed | tf_op | source)
XLA Modules:
  0.0 30.3 jit_solution(12286744027977182352)
XLA Ops:
  0.0 29.6 %shard_map.73 = bf16[4,4,4096]{2,1,0:T(4,128)(2,1)S(1)} custom-call(bf16[4,4096]{1,0:T(4,128)(2,1)} %tok_hbm.1, s32[2,4]{1,0:T(2,128)} %bitcast.8, bf16[2,4]{1,0:T(2,128)(2,1)} %bitcast.9, s32[2,2]{1,0:T(2,128)} %placement_hbm.1, bf16[384,4096]{1,0:T(8,128)(2,1)} %bitcast.5, bf16[384,4096]{1,0:T(8,128)(2,1)} %bitcast.6, bf16[384,4096]{1,0:T(8,128)(2,1)} %bitcast.7), custom_call_target="tpu_custom_call" | custom-call | tf_op jit(solution)/shard_map/pallas_call | solution.py:569
  29.7 0.7 %reduce_sum.12 = bf16[4,4096]{1,0:T(4,128)(2,1)} reduce(bf16[4,4,4096]{2,1,0:T(4,128)(2,1)S(1)} %shard_map.73, bf16[]{:T(256)} %constant.2.clone.1), dimensions={0}, to_apply=%region_0.0 | reduce | flops 49152 | bytes 163842 | tf_op jit(solution)/shard_map/reduce_sum | solution.py:602

commit v4 on v3

--- a/solution.py
+++ b/solution.py
@@ -275,7 +275,7 @@
 
 def relay_kernel(experts, dp, topk, first, slots, pad, bands, cuts,
                  tok_hbm, ids_hbm, gates_hbm, placement_hbm, wg_hbm, wu_hbm, wd_hbm, out,
-                 ids, gates, placement, rows, flat, wgu, wd, acc, hid, part_s, part_r, back_s,
+                 ids, gates, placement, rows, flat, wgu, wd, acc, hid, partial, part_s, part_r, back_s,
                  ready_e, ready_d, l_sem, w_sem, z_s, z_r, d_s, d_r, f_s, c_s, c_r, h_sem, p_s, p_r, b_s, b_r):
     me_e = lax.axis_index("expert")
     me_j = lax.axis_index("dp")
@@ -325,8 +325,11 @@
     def left(ref, sem):
         to_expert(ref, ref, sem, sem, sibling).wait_send()
 
+    mid = bands // 2
+    split = mid * band
+
     def edge(b):
-        return 0 if b == 0 else pad + b * band
+        return b * band + (pad if b > mid else 0)
 
     def cols(b0, b1):
         return pl.ds(edge(b0), edge(b1) - edge(b0))
@@ -364,7 +367,8 @@
     given = pl.ds(pl.multiple_of((1 - core) * half, 128), half)
     loads = [pltpu.make_async_copy(a, b, l_sem.at[i]) for i, (a, b) in enumerate((
         (ids_hbm, ids), (gates_hbm, gates), (placement_hbm, placement),
-        (tok_hbm, mine.at[:, pl.ds(pad, width)]),
+        (tok_hbm.at[:, pl.ds(0, split)], mine.at[:, pl.ds(0, split)]),
+        (tok_hbm.at[:, pl.ds(split, width - split)], mine.at[:, pl.ds(split + pad, width - split)]),
         (wg_hbm, wgu.at[pl.ds(0, units)]), (wu_hbm, wgu.at[pl.ds(units, units)]),
         (wd_hbm.at[:, kept], wd.at[core])))]
     for load in loads:
@@ -375,6 +379,27 @@
             pl.when(q < z)(functools.partial(tell, ready_e.at[z - 1, core], "expert", q * 2 + o))
     for s in range(1, dp):
         pl.when(across[s] < me_j)(functools.partial(tell, ready_d.at[s - 1], "dp", across[s]))
+
+    def far_send(n, src, c, part):
+        other = sent_to(n)
+        k = seen_from(other)
+        to_expert(src, rows.at[core, k, me_j, :, c], z_s, z_r.at[k - 1, part], other * 2 + core).start()
+
+    def send_tokens(n):
+        far_send(n, tok_hbm.at[:, pl.ds(0, split)], pl.ds(0, split), 0)
+        far_send(n, tok_hbm.at[:, pl.ds(split, width - split)], pl.ds(split + pad, width - split), 1)
+
+    told_at = pl.ds(split, pad)
+
+    def send_all(n):
+        for part, c in enumerate((pl.ds(0, split), pl.ds(split, width + pad - split))):
+            far_send(n, mine.at[:, c], c, part)
+
+    def send_told(n):
+        far_send(n, mine.at[:, told_at], told_at, 1)
+
+    for n in range(chips - 1):
+        pl.when(n < z)(functools.partial(send_tokens, n))
 
     for load in loads[:3]:
         load.wait()
@@ -388,8 +413,11 @@
             for at, table in ((k, id_f), (topk + k, gate_f)):
                 here = jnp.where(line == t, lane, -1) == at
                 info = jnp.where(here, jnp.broadcast_to(table[k:k + 1, t:t + 1], (own, pad)), info)
-    rows[core, 0, me_j, :, 0:pad] = info.astype(BF16)
+    rows[core, 0, me_j, :, told_at] = info.astype(BF16)
+    for n in range(chips - 1):
+        pl.when(n < z)(functools.partial(send_told, n))
     loads[3].wait()
+    loads[4].wait()
 
     def over_dp(k, i, s, at):
         here = rows.at[core, k, at, :, cols(*cuts[k][i])]
@@ -399,12 +427,10 @@
         meet_dp(s)
         over_dp(0, 0, s, me_j).start()
     for n in range(chips - 1):
-        other = sent_to(n)
-        k = seen_from(other)
-        meet_chip(other, core)
-        for i in range(len(z_cuts)):
-            c = cols(*z_cuts[i])
-            to_expert(mine.at[:, c], rows.at[core, k, me_j, :, c], z_s, z_r.at[k - 1, i], other * 2 + core).start()
+        @pl.when(n >= z)
+        def _():
+            meet_chip(sent_to(n), core)
+            send_all(n)
     lend = to_expert(wd_hbm.at[:, given], wd.at[core], w_sem.at[0], w_sem.at[1], sibling)
     lend.start()
 
@@ -459,17 +485,17 @@
                 spread(k - 1, i)
 
     contract = (((1,), (1,)), ((), ()))
-    loads[4].wait()
     loads[5].wait()
+    loads[6].wait()
     me_f = me_e.astype(F32)
     weight = None
     for b in range(bands):
         for i, (b0, b1) in enumerate(cuts[far]):
             if b0 == b:
                 spread(far, i)
-        x = flat[:, pl.ds(pad + b * band, band)].astype(BF16)
+        x = flat[:, pl.ds(b * band + (pad if b >= mid else 0), band)].astype(BF16)
         total = lax.dot_general(x, wgu[:, pl.ds(b * band, band)], contract, preferred_element_type=F32)
-        if b == 0:
+        if b == mid:
             r = lax.broadcasted_iota(jnp.int32, (many, many), 0)
             q = lax.broadcasted_iota(jnp.int32, (many, many), 1)
             of_r = jnp.where(lax.div(r, span) == lax.div(q, span), lax.rem(lax.div(r, own), 2), 2)
@@ -477,7 +503,7 @@
             below = jnp.where(same, jnp.where(q < r, 1.0, 0.0), 0.0).astype(BF16)
             listed = placement[0:1, :].astype(F32)
             extra = jnp.sum(jnp.where(listed == me_f, float(slots - first), 0.0), axis=1, keepdims=True)
-            told = flat[:, 0:pad]
+            told = flat[:, told_at]
             named = jnp.zeros((many, 1), F32)
             value = jnp.zeros((many, 1), F32)
             for k in range(topk):
@@ -486,6 +512,7 @@
                 value = value + jnp.where(hit, told[:, topk + k:topk + k + 1], 0.0)
             rank = jnp.dot(below, jnp.broadcast_to(named, (many, 128)).astype(BF16), preferred_element_type=F32)[:, 0:1]
             weight = jnp.where(rank < float(first) + extra, value, 0.0)
+        if b == 0:
             acc[...] = total
         elif b < bands - 1:
             acc[...] += total
@@ -496,7 +523,11 @@
 
     swap = to_expert(hid.at[core], hid.at[core], h_sem.at[0], h_sem.at[1], sibling)
     swap.start()
-    loads[6].wait()
+    loads[7].wait()
+    piece = half // bands
+    for b in range(bands):
+        c = pl.ds(b * piece, piece)
+        partial[:, c] = jnp.dot(hid[core], wd[core, :, c], preferred_element_type=F32)
     landed(wd.at[1 - core], w_sem.at[1])
     landed(hid.at[1 - core], h_sem.at[1])
 
@@ -504,15 +535,14 @@
         for s in reversed(range(1, dp)):
             to_dp(part_s.at[k * dp + across[s], :, c], part_r.at[k, s - 1, :, c], p_s.at[k], p_r.at[k], s).start()
 
-    piece = half // bands
     for b in range(bands):
         c = pl.ds(b * piece, piece)
-        total = jnp.dot(hid[0], wd[0, :, c], preferred_element_type=F32)
-        total = total + jnp.dot(hid[1], wd[1, :, c], preferred_element_type=F32)
+        total = partial[:, c] + jnp.dot(hid[1 - core], wd[1 - core, :, c], preferred_element_type=F32)
         part_s[:, :, c] = total.reshape(chips * dp, both, piece).astype(BF16)
-        send_part(far, c)
-    for k in reversed(range(far)):
-        send_part(k, pl.ds(0, half))
+        send_part(3, c)
+    send_part(2, pl.ds(0, half))
+    send_part(1, pl.ds(0, half))
+    send_part(0, pl.ds(0, half))
     for k in range(1, chips):
         meet_chip(chip_at(k), 1 - core)
 
@@ -542,7 +572,8 @@
         else:
             left(here, d_s.at[k])
         left(rows.at[core, k], c_s.at[k])
-        left(part_r.at[k], p_s.at[k])
+        if k not in ():
+            left(part_r.at[k], p_s.at[k])
     keep.wait()
     give.wait_send()
     left(out.at[pl.ds(0, chips - 1)], b_s.at[0])
@@ -581,11 +612,12 @@
             pltpu.VMEM((2, units, half), BF16),
             pltpu.VMEM((many, 2 * units), F32),
             pltpu.VMEM((2, many, units), BF16),
+            pltpu.VMEM((many, half), F32),
             pltpu.VMEM((chips * dp, 2 * own, half), BF16),
             pltpu.VMEM((chips, dp - 1, 2 * own, half), BF16),
             pltpu.VMEM((chips, 2, own, half), BF16),
             pltpu.SemaphoreType.REGULAR((chips - 1, 2)), pltpu.SemaphoreType.REGULAR((dp - 1,)),
-            dma((7,)),
+            dma((8,)),
             dma((2,)),
             dma, dma((chips - 1, 2)),
             dma((chips,)), dma((parts_of,)),

time: 30.5 us -> 30.1 us (0.987)
    pallas_call x1, Pallas kernels: 29.6 us -> 29.3 us  [relayed(): pl.pallas_call(functools.partial(relay_kernel, experts, dp, topk, first,...]
where the time goes in v4:
time: 30.1 us; the launch traced here: 30 us
  Pallas kernels  29.3 us (97%)
  other arithmetic  0.68 us (2%)
    pallas_call x1, Pallas kernels, relayed(): pl.pallas_call(functools.partial(relay_kernel, experts, dp, topk, first,...  29.3 us
    reduce_sum x1, other arithmetic, relayed(): return jnp.sum(parts.astype(F32), axis=0).astype(BF16)  0.68 us

profile of v4, /device:TPU:0, one launch (start us, length us, event | category | flops | bytes accessed | tf_op | source)
XLA Modules:
  0.0 30.0 jit_solution(727625751616399465)
XLA Ops:
  0.0 29.3 %shard_map.73 = bf16[4,4,4096]{2,1,0:T(4,128)(2,1)S(1)} custom-call(bf16[4,4096]{1,0:T(4,128)(2,1)} %tok_hbm.1, s32[2,4]{1,0:T(2,128)} %bitcast.8, bf16[2,4]{1,0:T(2,128)(2,1)} %bitcast.9, s32[2,2]{1,0:T(2,128)} %placement_hbm.1, bf16[384,4096]{1,0:T(8,128)(2,1)} %bitcast.5, bf16[384,4096]{1,0:T(8,128)(2,1)} %bitcast.6, bf16[384,4096]{1,0:T(8,128)(2,1)} %bitcast.7), custom_call_target="tpu_custom_call" | custom-call | tf_op jit(solution)/shard_map/pallas_call | solution.py:600
  29.3 0.7 %reduce_sum.12 = bf16[4,4096]{1,0:T(4,128)(2,1)} reduce(bf16[4,4,4096]{2,1,0:T(4,128)(2,1)S(1)} %shard_map.73, bf16[]{:T(256)} %constant.2.clone.1), dimensions={0}, to_apply=%region_0.0 | reduce | flops 49152 | bytes 163842 | tf_op jit(solution)/shard_map/reduce_sum | solution.py:634

commit v5 on v4

--- a/solution.py
+++ b/solution.py
@@ -275,8 +275,8 @@
 
 def relay_kernel(experts, dp, topk, first, slots, pad, bands, cuts,
                  tok_hbm, ids_hbm, gates_hbm, placement_hbm, wg_hbm, wu_hbm, wd_hbm, out,
-                 ids, gates, placement, rows, flat, wgu, wd, acc, hid, partial, part_s, part_r, back_s,
-                 ready_e, ready_d, l_sem, w_sem, z_s, z_r, d_s, d_r, f_s, c_s, c_r, h_sem, p_s, p_r, b_s, b_r):
+                 ids, gates, placement, rows, flat, wgu, wd, acc, hid, partial, part_s, part_r, diag_r, back_s,
+                 ready_e, ready_d, l_sem, w_sem, z_s, z_r, d_s, d_r, g_s, g_r, c_s, c_r, h_sem, p_s, p_r, q_s, q_r, b_s, b_r):
     me_e = lax.axis_index("expert")
     me_j = lax.axis_index("dp")
     core = lax.rem(me_e, 2)
@@ -371,7 +371,7 @@
         (tok_hbm.at[:, pl.ds(split, width - split)], mine.at[:, pl.ds(split + pad, width - split)]),
         (wg_hbm, wgu.at[pl.ds(0, units)]), (wu_hbm, wgu.at[pl.ds(units, units)]),
         (wd_hbm.at[:, kept], wd.at[core])))]
-    for load in loads:
+    for load in loads[:5]:
         load.start()
     pl.semaphore_wait(barrier, 1 + 2 * z + me_j)
     for q in range(chips - 1):
@@ -400,6 +400,8 @@
 
     for n in range(chips - 1):
         pl.when(n < z)(functools.partial(send_tokens, n))
+    for load in loads[5:]:
+        load.start()
 
     for load in loads[:3]:
         load.wait()
@@ -440,18 +442,29 @@
                 if b0 <= a0 < b1:
                     landed(rows.at[core, k, me_j, :, cols(a0, a1)], z_r.at[k - 1, n])
 
-            def onward():
-                for s in range(1, dp):
-                    over_dp(k, i, s, me_j).start()
-
-            if k == far:
-                pl.when(z != far)(onward)
-            else:
-                onward()
+            for s in range(1, dp - 1):
+                over_dp(k, i, s, me_j).start()
+
+            @pl.when(chip_at(k) > z)
+            def _():
+                over_dp(k, i, dp - 1, me_j).start()
 
     def share(k, i):
         c = cols(*cuts[k][i])
-        landed(rows.at[core, k, pl.ds(0, dp - 1), :, c], d_r.at[at_cut[k, i]])
+
+        def wait_for(count):
+            landed(rows.at[core, k, pl.ds(0, count), :, c], d_r.at[at_cut[k, i]])
+
+        if k == 0:
+            wait_for(dp - 1)
+        else:
+            pl.when(chip_at(k) > z)(functools.partial(wait_for, dp - 1))
+
+            @pl.when(chip_at(k) < z)
+            def _():
+                wait_for(dp - 2)
+                if i == 0:
+                    landed(rows.at[core, k, 0], g_r.at[k - 1])
         here = rows.at[core, k, :, :, c]
         to_expert(here, here, c_s.at[k], c_r.at[at_cut[k, i]], sibling).start()
 
@@ -463,19 +476,23 @@
                 start = k * span + j * both + o * own
                 flat[start:start + own, c] = rows[o, k, j, :, c].astype(F32)
 
+    def relay(n):
+        k = seen_from(sent_to(n))
+        return to_expert(rows.at[core, 0, across[dp - 1]], rows.at[core, k, across[dp - 1]], g_s.at[n], g_r.at[k - 1],
+                         sent_to(n) * 2 + core)
+
+    def share_own():
+        share(0, 0)
+        for n in range(chips - 1):
+            @pl.when(n >= z)
+            def _():
+                relay(n).start()
+
     pass_on(1)
-    share(0, 0)
-
-    @pl.when(z == 0)
-    def _():
-        for i in range(len(cuts[far])):
-            c = cols(*cuts[far][i])
-            for s in range(1, dp):
-                to_expert(rows.at[core, 0, across[s], :, c], rows.at[core, far, across[s], :, c], f_s,
-                          d_r.at[at_cut[far, i]], far * 2 + core).start()
-
+    pl.when(z == 0)(share_own)
     for k in range(2, chips):
         pass_on(k)
+    pl.when(z != 0)(share_own)
     spread(0, 0)
     for k in range(1, chips):
         for i in range(len(cuts[k])):
@@ -531,31 +548,86 @@
     landed(wd.at[1 - core], w_sem.at[1])
     landed(hid.at[1 - core], h_sem.at[1])
 
+    ends = z * (far - z) == 0
+    diagonal = dp - 1
+
     def send_part(k, c):
-        for s in reversed(range(1, dp)):
+        for s in range(1, diagonal):
             to_dp(part_s.at[k * dp + across[s], :, c], part_r.at[k, s - 1, :, c], p_s.at[k], p_r.at[k], s).start()
 
+    def send_far_diagonal(c):
+        to_dp(part_s.at[far * dp + across[diagonal], :, c], part_r.at[far, diagonal - 1, :, c], p_s.at[chips],
+              p_r.at[chips], diagonal).start()
+
+    def send_over_z(k, c):
+        other = chip_at(k)
+        at = seen_from(other) - 1
+        to_expert(part_s.at[k * dp + across[diagonal], :, c], diag_r.at[at, :, c], q_s.at[lax.div(k, far)], q_r.at[at],
+                  other * 2 + core).start()
+
+    def rest(b):
+        return jnp.dot(hid[1 - core], wd[1 - core, :, b * piece:(b + 1) * piece], preferred_element_type=F32)
+
+    ahead = rest(0)
     for b in range(bands):
         c = pl.ds(b * piece, piece)
-        total = partial[:, c] + jnp.dot(hid[1 - core], wd[1 - core, :, c], preferred_element_type=F32)
+        total = partial[:, c] + ahead
+        if b < bands - 1:
+            ahead = rest(b + 1)
         part_s[:, :, c] = total.reshape(chips * dp, both, piece).astype(BF16)
-        send_part(3, c)
-    send_part(2, pl.ds(0, half))
-    send_part(1, pl.ds(0, half))
-    send_part(0, pl.ds(0, half))
+        send_part(far, c)
+        if b % 2 == 1:
+            c = pl.ds((b - 1) * piece, 2 * piece)
+            pl.when(ends)(functools.partial(send_far_diagonal, c))
+            pl.when(jnp.logical_not(ends))(functools.partial(send_over_z, far, c))
+            for k in range(1, far):
+                send_over_z(k, c)
+    for k in reversed(range(far)):
+        send_part(k, pl.ds(0, half))
     for k in range(1, chips):
         meet_chip(chip_at(k), 1 - core)
 
-    for k in reversed(range(chips)):
+    def pack(to, value):
+        for o in range(2):
+            to[o] = value[o * own:(o + 1) * own, :].astype(BF16)
+
+    def gather_part(k):
+        landed(part_r.at[k, pl.ds(0, diagonal - 1)], p_r.at[k])
         value = part_s[k * dp + me_j].astype(F32)
-        landed(part_r.at[k], p_r.at[k])
-        for s in range(dp - 1):
+        for s in range(diagonal - 1):
             value = value + part_r[k, s].astype(F32)
-        for o in range(2):
-            back_s[k, o] = value[o * own:(o + 1) * own, :].astype(BF16)
+        pack(back_s.at[k], value)
+        if k == far:
+            @pl.when(ends)
+            def _():
+                landed(part_r.at[far, diagonal - 1], p_r.at[chips])
+                pack(back_s.at[k], value + part_r[far, diagonal - 1].astype(F32))
         if k > 0:
             for o in range(2):
                 to_expert(back_s.at[k, o], out.at[z, :, kept], b_s.at[0], b_r.at[0], chip_at(k) * 2 + o).start()
+
+    def gather_diagonal():
+        value = part_s[across[diagonal]].astype(F32)
+        for k in range(1, far):
+            landed(diag_r.at[k - 1], q_r.at[k - 1])
+            value = value + diag_r[k - 1].astype(F32)
+        pack(back_s.at[chips], value)
+
+        @pl.when(jnp.logical_not(ends))
+        def _():
+            landed(diag_r.at[far - 1], q_r.at[far - 1])
+            pack(back_s.at[chips], value + diag_r[far - 1].astype(F32))
+
+        for o in range(2):
+            pltpu.make_async_remote_copy(
+                src_ref=back_s.at[chips, o], dst_ref=out.at[chips, :, kept], send_sem=b_s.at[3], recv_sem=b_r.at[2],
+                device_id={"expert": z * 2 + o, "dp": across[diagonal]}, device_id_type=MESH).start()
+
+    gather_part(3)
+    gather_part(2)
+    gather_diagonal()
+    gather_part(1)
+    gather_part(0)
     give = to_expert(back_s.at[0, 1 - core], out.at[z, :, kept], b_s.at[1], b_r.at[1], sibling)
     give.start()
     keep = pltpu.make_async_copy(back_s.at[0, core], out.at[z, :, kept], b_s.at[2])
@@ -565,17 +637,22 @@
     swap.wait_send()
     left(rows.at[core, 0, pl.ds(0, chips - 1)], z_s)
     for k in range(chips):
-        here = rows.at[core, k, pl.ds(0, dp - 1)]
-        if k == far:
-            pl.when(z != far)(functools.partial(left, here, d_s.at[k]))
-            pl.when(z == 0)(functools.partial(left, here, f_s))
+        if k == 0:
+            left(rows.at[core, k, pl.ds(0, dp - 1)], d_s.at[k])
         else:
-            left(here, d_s.at[k])
+            pl.when(chip_at(k) > z)(functools.partial(left, rows.at[core, k, pl.ds(0, dp - 1)], d_s.at[k]))
+            pl.when(chip_at(k) < z)(functools.partial(left, rows.at[core, k, pl.ds(0, dp - 2)], d_s.at[k]))
+            pl.when(k > z)(functools.partial(left, rows.at[core, 0, 0], g_s.at[k - 1]))
         left(rows.at[core, k], c_s.at[k])
         if k not in ():
-            left(part_r.at[k], p_s.at[k])
+            left(part_r.at[k, pl.ds(0, diagonal - 1)], p_s.at[k])
     keep.wait()
     give.wait_send()
+    left(diag_r.at[pl.ds(0, far - 1)], q_s.at[0])
+    pl.when(ends)(functools.partial(left, diag_r.at[0], p_s.at[chips]))
+    pl.when(jnp.logical_not(ends))(functools.partial(left, diag_r.at[0], q_s.at[1]))
+    left(out.at[chips], b_s.at[3])
+    landed(out.at[chips], b_r.at[2])
     left(out.at[pl.ds(0, chips - 1)], b_s.at[0])
     landed(out.at[z, :, given], b_r.at[1])
     landed(out.at[pl.ds(0, chips - 1)], b_r.at[0])
@@ -599,7 +676,7 @@
     dma = pltpu.SemaphoreType.DMA
     parts = pl.pallas_call(
         functools.partial(relay_kernel, experts, dp, topk, first, slots, pad, bands, cuts),
-        out_shape=pltpu.VMEM((chips, own, width), BF16),
+        out_shape=pltpu.VMEM((chips + 1, own, width), BF16),
         in_specs=[hbm] * 7,
         out_specs=pl.BlockSpec(memory_space=pltpu.VMEM),
         scratch_shapes=[
@@ -615,17 +692,19 @@
             pltpu.VMEM((many, half), F32),
             pltpu.VMEM((chips * dp, 2 * own, half), BF16),
             pltpu.VMEM((chips, dp - 1, 2 * own, half), BF16),
-            pltpu.VMEM((chips, 2, own, half), BF16),
+            pltpu.VMEM((chips - 1, 2 * own, half), BF16),
+            pltpu.VMEM((chips + 1, 2, own, half), BF16),
             pltpu.SemaphoreType.REGULAR((chips - 1, 2)), pltpu.SemaphoreType.REGULAR((dp - 1,)),
             dma((8,)),
             dma((2,)),
             dma, dma((chips - 1, 2)),
             dma((chips,)), dma((parts_of,)),
-            dma,
+            dma((chips - 1,)), dma((chips - 1,)),
             dma((chips,)), dma((parts_of,)),
             dma((2,)),
-            dma((chips,)), dma((chips,)),
-            dma((3,)), dma((2,)),
+            dma((chips + 1,)), dma((chips + 1,)),
+            dma((2,)), dma((chips - 1,)),
+            dma((4,)), dma((3,)),
         ],
         compiler_params=pltpu.CompilerParams(
             collective_id=1, has_side_effects=True, vmem_limit_bytes=56 << 20

time: 30.1 us -> 28.9 us (0.960)
  Pallas kernels: 29.3 us -> 28 us
    pallas_call x1, Pallas kernels: 29.3 us -> 28 us  [relayed(): pl.pallas_call(functools.partial(relay_kernel, experts, dp, topk, first,...]
where the time goes in v5:
time: 28.9 us; the launch traced here: 28.7 us
  Pallas kernels  28 us (97%)
  other arithmetic  0.7 us (2%)
    pallas_call x1, Pallas kernels, relayed(): pl.pallas_call(functools.partial(relay_kernel, experts, dp, topk, first,...  28 us
    reduce_sum x1, other arithmetic, relayed(): return jnp.sum(parts.astype(F32), axis=0).astype(BF16)  0.7 us

profile of v5, /device:TPU:0, one launch (start us, length us, event | category | flops | bytes accessed | tf_op | source)
XLA Modules:
  0.0 28.7 jit_solution(15263007048286780403)
XLA Ops:
  0.0 28.0 %shard_map.73 = bf16[5,4,4096]{2,1,0:T(4,128)(2,1)S(1)} custom-call(bf16[4,4096]{1,0:T(4,128)(2,1)} %tok_hbm.1, s32[2,4]{1,0:T(2,128)} %bitcast.8, bf16[2,4]{1,0:T(2,128)(2,1)} %bitcast.9, s32[2,2]{1,0:T(2,128)} %placement_hbm.1, bf16[384,4096]{1,0:T(8,128)(2,1)} %bitcast.5, bf16[384,4096]{1,0:T(8,128)(2,1)} %bitcast.6, bf16[384,4096]{1,0:T(8,128)(2,1)} %bitcast.7), custom_call_target="tpu_custom_call" | custom-call | tf_op jit(solution)/shard_map/pallas_call | solution.py:677
  28.0 0.7 %reduce_sum.12 = bf16[4,4096]{1,0:T(4,128)(2,1)} reduce(bf16[5,4,4096]{2,1,0:T(4,128)(2,1)S(1)} %shard_map.73, bf16[]{:T(256)} %constant.2.clone.1), dimensions={0}, to_apply=%region_0.0 | reduce | flops 65536 | bytes 196610 | tf_op jit(solution)/shard_map/reduce_sum | solution.py:713

commit v6 on v5

--- a/solution.py
+++ b/solution.py
@@ -548,21 +548,16 @@
     landed(wd.at[1 - core], w_sem.at[1])
     landed(hid.at[1 - core], h_sem.at[1])
 
-    ends = z * (far - z) == 0
     diagonal = dp - 1
 
     def send_part(k, c):
         for s in range(1, diagonal):
             to_dp(part_s.at[k * dp + across[s], :, c], part_r.at[k, s - 1, :, c], p_s.at[k], p_r.at[k], s).start()
 
-    def send_far_diagonal(c):
-        to_dp(part_s.at[far * dp + across[diagonal], :, c], part_r.at[far, diagonal - 1, :, c], p_s.at[chips],
-              p_r.at[chips], diagonal).start()
-
     def send_over_z(k, c):
         other = chip_at(k)
         at = seen_from(other) - 1
-        to_expert(part_s.at[k * dp + across[diagonal], :, c], diag_r.at[at, :, c], q_s.at[lax.div(k, far)], q_r.at[at],
+        to_expert(part_s.at[k * dp + across[diagonal], :, c], diag_r.at[at, :, c], q_s, q_r.at[at],
                   other * 2 + core).start()
 
     def rest(b):
@@ -576,12 +571,9 @@
             ahead = rest(b + 1)
         part_s[:, :, c] = total.reshape(chips * dp, both, piece).astype(BF16)
         send_part(far, c)
-        if b % 2 == 1:
-            c = pl.ds((b - 1) * piece, 2 * piece)
-            pl.when(ends)(functools.partial(send_far_diagonal, c))
-            pl.when(jnp.logical_not(ends))(functools.partial(send_over_z, far, c))
-            for k in range(1, far):
-                send_over_z(k, c)
+        send_over_z(far, c)
+    for k in reversed(range(1, far)):
+        send_over_z(k, pl.ds(0, half))
     for k in reversed(range(far)):
         send_part(k, pl.ds(0, half))
     for k in range(1, chips):
@@ -597,26 +589,16 @@
         for s in range(diagonal - 1):
             value = value + part_r[k, s].astype(F32)
         pack(back_s.at[k], value)
-        if k == far:
-            @pl.when(ends)
-            def _():
-                landed(part_r.at[far, diagonal - 1], p_r.at[chips])
-                pack(back_s.at[k], value + part_r[far, diagonal - 1].astype(F32))
         if k > 0:
             for o in range(2):
                 to_expert(back_s.at[k, o], out.at[z, :, kept], b_s.at[0], b_r.at[0], chip_at(k) * 2 + o).start()
 
     def gather_diagonal():
         value = part_s[across[diagonal]].astype(F32)
-        for k in range(1, far):
+        for k in range(1, chips):
             landed(diag_r.at[k - 1], q_r.at[k - 1])
             value = value + diag_r[k - 1].astype(F32)
         pack(back_s.at[chips], value)
-
-        @pl.when(jnp.logical_not(ends))
-        def _():
-            landed(diag_r.at[far - 1], q_r.at[far - 1])
-            pack(back_s.at[chips], value + diag_r[far - 1].astype(F32))
 
         for o in range(2):
             pltpu.make_async_remote_copy(
@@ -625,8 +607,8 @@
 
     gather_part(3)
     gather_part(2)
+    gather_part(1)
     gather_diagonal()
-    gather_part(1)
     gather_part(0)
     give = to_expert(back_s.at[0, 1 - core], out.at[z, :, kept], b_s.at[1], b_r.at[1], sibling)
     give.start()
@@ -648,9 +630,7 @@
             left(part_r.at[k, pl.ds(0, diagonal - 1)], p_s.at[k])
     keep.wait()
     give.wait_send()
-    left(diag_r.at[pl.ds(0, far - 1)], q_s.at[0])
-    pl.when(ends)(functools.partial(left, diag_r.at[0], p_s.at[chips]))
-    pl.when(jnp.logical_not(ends))(functools.partial(left, diag_r.at[0], q_s.at[1]))
+    left(diag_r, q_s)
     left(out.at[chips], b_s.at[3])
     landed(out.at[chips], b_r.at[2])
     left(out.at[pl.ds(0, chips - 1)], b_s.at[0])
@@ -691,7 +671,7 @@
             pltpu.VMEM((2, many, units), BF16),
             pltpu.VMEM((many, half), F32),
             pltpu.VMEM((chips * dp, 2 * own, half), BF16),
-            pltpu.VMEM((chips, dp - 1, 2 * own, half), BF16),
+            pltpu.VMEM((chips, dp - 2, 2 * own, half), BF16),
             pltpu.VMEM((chips - 1, 2 * own, half), BF16),
             pltpu.VMEM((chips + 1, 2, own, half), BF16),
             pltpu.SemaphoreType.REGULAR((chips - 1, 2)), pltpu.SemaphoreType.REGULAR((dp - 1,)),
@@ -702,8 +682,8 @@
             dma((chips - 1,)), dma((chips - 1,)),
             dma((chips,)), dma((parts_of,)),
             dma((2,)),
-            dma((chips + 1,)), dma((chips + 1,)),
-            dma((2,)), dma((chips - 1,)),
+            dma((chips,)), dma((chips,)),
+            dma, dma((chips - 1,)),
             dma((4,)), dma((3,)),
         ],
         compiler_params=pltpu.CompilerParams(

time: 28.9 us -> 28.2 us (0.976)
  Pallas kernels: 28 us -> 27.3 us
    pallas_call x1, Pallas kernels: 28 us -> 27.3 us  [relayed(): pl.pallas_call(functools.partial(relay_kernel, experts, dp, topk, first,...]
where the time goes in v6:
time: 28.2 us; the launch traced here: 28 us
  Pallas kernels  27.3 us (97%)
  other arithmetic  0.7 us (2%)
    pallas_call x1, Pallas kernels, relayed(): pl.pallas_call(functools.partial(relay_kernel, experts, dp, topk, first,...  27.3 us
    reduce_sum x1, other arithmetic, relayed(): return jnp.sum(parts.astype(F32), axis=0).astype(BF16)  0.7 us

profile of v6, /device:TPU:0, one launch (start us, length us, event | category | flops | bytes accessed | tf_op | source)
XLA Modules:
  0.0 28.0 jit_solution(6641511278215400090)
XLA Ops:
  0.0 27.3 %shard_map.73 = bf16[5,4,4096]{2,1,0:T(4,128)(2,1)S(1)} custom-call(bf16[4,4096]{1,0:T(4,128)(2,1)} %tok_hbm.1, s32[2,4]{1,0:T(2,128)} %bitcast.8, bf16[2,4]{1,0:T(2,128)(2,1)} %bitcast.9, s32[2,2]{1,0:T(2,128)} %placement_hbm.1, bf16[384,4096]{1,0:T(8,128)(2,1)} %bitcast.5, bf16[384,4096]{1,0:T(8,128)(2,1)} %bitcast.6, bf16[384,4096]{1,0:T(8,128)(2,1)} %bitcast.7), custom_call_target="tpu_custom_call" | custom-call | tf_op jit(solution)/shard_map/pallas_call | solution.py:657
  27.3 0.7 %reduce_sum.12 = bf16[4,4096]{1,0:T(4,128)(2,1)} reduce(bf16[5,4,4096]{2,1,0:T(4,128)(2,1)S(1)} %shard_map.73, bf16[]{:T(256)} %constant.2.clone.1), dimensions={0}, to_apply=%region_0.0 | reduce | flops 65536 | bytes 196610 | tf_op jit(solution)/shard_map/reduce_sum | solution.py:693

commit v7 on v6

--- a/solution.py
+++ b/solution.py
@@ -608,13 +608,12 @@
     gather_part(3)
     gather_part(2)
     gather_part(1)
-    gather_diagonal()
     gather_part(0)
     give = to_expert(back_s.at[0, 1 - core], out.at[z, :, kept], b_s.at[1], b_r.at[1], sibling)
     give.start()
     keep = pltpu.make_async_copy(back_s.at[0, core], out.at[z, :, kept], b_s.at[2])
     keep.start()
-
+    gather_diagonal()
     lend.wait_send()
     swap.wait_send()
     left(rows.at[core, 0, pl.ds(0, chips - 1)], z_s)
@@ -650,7 +649,7 @@
     whole = ((0, bands),)
     halves = ((0, bands // 2), (bands // 2, bands))
     single = tuple((b, b + 1) for b in range(bands))
-    cuts = tuple(single if k == chips - 1 else halves if k == chips - 2 else whole for k in range(chips))
+    cuts = tuple(single if k >= chips - 2 else whole for k in range(chips))
     parts_of = sum(len(c) for c in cuts)
     hbm = pl.BlockSpec(memory_space=pl.ANY)
     dma = pltpu.SemaphoreType.DMA

time: 28.2 us -> 28.2 us (level)
  no operation moved by 1% of the time
where the time goes in v7:
time: 28.2 us; the launch traced here: 28 us
  Pallas kernels  27.3 us (97%)
  other arithmetic  0.7 us (2%)
    pallas_call x1, Pallas kernels, relayed(): pl.pallas_call(functools.partial(relay_kernel, experts, dp, topk, first,...  27.3 us
    reduce_sum x1, other arithmetic, relayed(): return jnp.sum(parts.astype(F32), axis=0).astype(BF16)  0.7 us

profile of v7, /device:TPU:0, one launch (start us, length us, event | category | flops | bytes accessed | tf_op | source)
XLA Modules:
  0.0 28.0 jit_solution(9724283515804835306)
XLA Ops:
  0.0 27.3 %shard_map.73 = bf16[5,4,4096]{2,1,0:T(4,128)(2,1)S(1)} custom-call(bf16[4,4096]{1,0:T(4,128)(2,1)} %tok_hbm.1, s32[2,4]{1,0:T(2,128)} %bitcast.8, bf16[2,4]{1,0:T(2,128)(2,1)} %bitcast.9, s32[2,2]{1,0:T(2,128)} %placement_hbm.1, bf16[384,4096]{1,0:T(8,128)(2,1)} %bitcast.5, bf16[384,4096]{1,0:T(8,128)(2,1)} %bitcast.6, bf16[384,4096]{1,0:T(8,128)(2,1)} %bitcast.7), custom_call_target="tpu_custom_call" | custom-call | tf_op jit(solution)/shard_map/pallas_call | solution.py:656
  27.3 0.7 %reduce_sum.12 = bf16[4,4096]{1,0:T(4,128)(2,1)} reduce(bf16[5,4,4096]{2,1,0:T(4,128)(2,1)S(1)} %shard_map.73, bf16[]{:T(256)} %constant.2.clone.1), dimensions={0}, to_apply=%region_0.0 | reduce | flops 65536 | bytes 196610 | tf_op jit(solution)/shard_map/reduce_sum | solution.py:692
